TPU v7x, 256 devices: a whole 4x4x8 slice. The times are simulated.
256 devices in a mesh: tile: 32 (over z_hi, x, core), lev: 4 (over y), sec: 2 (over z_lo).
Axes of the slice: x: 4, y: 4, z: 8 (z_hi: 4, z_lo: 2; z = z_hi * 2 + z_lo), core: 2. Of those that a mesh axis runs over, the one named last changes fastest.
Arguments:
- forcing: float32 [8, 72, 1280, 384], P('sec', 'lev', 'tile'), may hold values from -6 to 6
- courant_x: bfloat16 [72, 1280, 384], P('lev', 'tile'), may hold values from -0.44921875 to 0.44921875
- courant_y: bfloat16 [72, 1280, 384], P('lev', 'tile'), may hold values from -0.44921875 to 0.44921875
- mass_flux: bfloat16 [72, 1280, 384], P('lev', 'tile'), may hold values from 0 to 0.59765625
- limiter_code: int32 [72, 1280, 384], P('lev', 'tile'), may hold values from 0 to 15
- seam_code: int32 [32, 2], replicated, may hold values from 0 to 1
- level_weight: float32 [72], P('lev'), may hold values from 0.02 to 0.5
- sector_share: float32 [8, 1280, 384], P('sec', 'tile'), may hold values from 0.1 to 1
- flux_cell: int32 [1024, 480], P('tile'), may hold values from 0 to 15359
Outputs:
- adjoint_start: float32 [8, 72, 1280, 384], P('sec', 'lev', 'tile')
- flux_sensitivity: float32 [491520], P('tile')
All inputs are finite; a program needn't handle non-finite values.
Results may differ from a plain program's by a relative error of at most 0.0003.
Values sent between devices are 32-bit elements; how exact they have to be, the bound alone decides.
A program may use at most 128 MiB of HBM per device.

v0:
```python
import jax
import jax.numpy as jnp
from jax import lax
from jax.sharding import PartitionSpec as P

FL_DEV = 15360


def from_behind(value, axis, steps):
    count = lax.axis_size(axis)
    initial, last = (max(0, -steps), min(count, count - steps))
    return lax.ppermute(value, axis, [(source, source + steps) for source in range(initial, last)])


def extended_2(value, sides, width):
    for axis, dim in sides:
        devices, length = (lax.axis_size(axis), value.shape[dim])
        up = [(i, (i + 1) % devices) for i in range(devices)]
        down = [(j, i) for i, j in up]
        last = lax.slice_in_dim(value, length - width, length, axis=dim)
        initial = lax.slice_in_dim(value, 0, width, axis=dim)
        before = lax.ppermute(last, axis, up)
        after = lax.ppermute(initial, axis, down)
        value = jnp.concatenate([before, value, after], axis=dim)
    return value


def coefficients(courant, codes, bit):
    value = courant.astype(jnp.float32)
    limited = jnp.bitwise_and(jnp.right_shift(codes, bit), 1).astype(jnp.float32)
    spread = 0.5 * jnp.abs(value) * (1.0 - jnp.abs(value))
    ahead = jnp.maximum(value, 0.0) - limited * spread
    behind = jnp.minimum(value, 0.0) + limited * spread
    return (ahead, behind)


def flipped(rim, flag):
    return jnp.where(flag, rim[..., ::-1], rim)


def vertical(adjoint, mixing, at_top):
    above = from_behind(adjoint[:, :1], "lev", -1)
    above = jnp.where(at_top, adjoint[:, -1:], above)
    upper = jnp.concatenate([adjoint[:, 1:], above], axis=1)
    return adjoint + mixing * (upper - adjoint)


def sweep_second(adjoint, courant, codes, bit):
    ahead, behind = coefficients(courant, codes, bit)
    following = jnp.concatenate([adjoint[..., 1:], adjoint[..., -1:]], axis=-1)
    previous = jnp.concatenate([adjoint[..., :1], adjoint[..., :-1]], axis=-1)
    return adjoint + ahead * (following - adjoint) + behind * (adjoint - previous)


def sweep_first(adjoint, courant, codes, bit, flip_left, flip_right):
    ahead, behind = coefficients(courant, codes, bit)
    extended = extended_2(adjoint, (("tile", 2),), 1)
    left_rim = flipped(extended[:, :, :1], flip_left)
    right_rim = flipped(extended[:, :, -1:], flip_right)
    following = jnp.concatenate([adjoint[:, :, 1:], right_rim], axis=2)
    previous = jnp.concatenate([left_rim, adjoint[:, :, :-1]], axis=2)
    return adjoint + ahead * (following - adjoint) + behind * (adjoint - previous)


def shards(
    forcing,
    courant_x,
    courant_y,
    mass_flux,
    limiter_code,
    seam_code,
    level_weight,
    sector_share,
    flux_cell,
):
    mixing = mass_flux.astype(jnp.float32)
    at_top = lax.axis_index("lev") == lax.axis_size("lev") - 1
    tile_count = lax.axis_size("tile")
    tile_rank = lax.axis_index("tile")
    place = jnp.remainder(tile_rank + tile_count, tile_count)
    seams_here = lax.dynamic_index_in_dim(seam_code, place, 0, keepdims=False) == 1
    adjoint = forcing
    for turn_index in (1, 0):
        adjoint = vertical(adjoint, mixing, at_top)
        adjoint = sweep_second(adjoint, courant_y, limiter_code, 2 * turn_index + 1)
        adjoint = sweep_first(
            adjoint, courant_x, limiter_code, 2 * turn_index, seams_here[0], seams_here[1]
        )
    partial_value = jnp.einsum(
        "sxy,l,slxy->xy", sector_share, level_weight, adjoint, precision=lax.Precision.HIGHEST
    )
    columns = partial_value.reshape(tile_count, -1)
    totals = lax.psum(columns, ("lev", "sec"))
    received = lax.all_to_all(totals, "tile", split_axis=0, concat_axis=0, tiled=True)
    flux_sensitivity = jax.ops.segment_sum(
        received.reshape(-1), flux_cell.reshape(-1), num_segments=FL_DEV
    )
    return (adjoint, flux_sensitivity)


def solution(mesh):
    placed = (
        P("sec", "lev", "tile", None),
        P("lev", "tile", None),
        P("lev", "tile", None),
        P("lev", "tile", None),
        P("lev", "tile", None),
        P(),
        P("lev"),
        P("sec", "tile", None),
        P("tile", None),
    )
    return jax.shard_map(
        shards,
        mesh=mesh,
        in_specs=placed,
        out_specs=(P("sec", "lev", "tile", None), P("tile")),
        check_vma=False,
    )
```

profile of v0, /device:TPU:1, one launch (start us, length us, event | category | flops | bytes accessed | tf_op | source)
XLA Modules:
  0.0 220.0 jit_solution(4765529639356526114)
XLA Ops:
  1.8 1.4 collective-permute-start
  3.2 5.8 %fusion.28 = (f32[18,40,384]{2,1,0:T(8,128)}, f32[18,40,384]{2,1,0:T(8,128)}, f32[18,40,384]{2,1,0:T(8,128)}, f32[18,40,384]{2,1,0:T(8,128)}, f32[18,40,384]{2,1...) fusion(bf16[18,40,384]{2,1,0:T(8,128)(2,1)} %param.10, ...), kind=kLoop, calls=%fused_computation.45 | loop fusion | flops 10506240 | bytes 11059200 | tf_op jit(solution)/shard_map/sub | solution.py:32
  9.0 2.3 %slice.76 = f32[4,17,40,384]{3,2,1,0:T(8,128)} slice(f32[4,18,40,384]{3,2,1,0:T(8,128)S(1)} %bitcast.18), slice={[0:4], [1:18], [0:40], [0:384]} | slice | bytes 8355840 | tf_op jit(solution)/shard_map/slice | solution.py:44
  13.0 4.2 %fusion.3 = f32[4,18,40,384]{3,2,1,0:T(8,128)S(1)} fusion(f32[4,18,40,384]{3,2,1,0:T(8,128)} %param.9, f32[4,1,40,384]{3,2,1,0:T(8,128)S(1)} %slice_select_fusion.1, f32[4,17,40,384]{3,2,1,0:T(8,128)} %slice.76, f32[18,40,384]{2,1,0:T(8,128)S(1)} %convert_element_type.23), kind=kLoop, calls=%fused_computation.5 | loop fusion | flops 4423680 | bytes 14376960 | tf_op jit(solution)/shard_map/add | solution.py:45
  17.2 1.6 fusion.46
  18.8 1.4 fusion.47
  20.2 3.7 %fusion.6 = f32[4,18,40,384]{3,2,1,0:T(8,128)S(1)} fusion(f32[4,18,40,384]{3,2,1,0:T(8,128)S(1)} %fusion.3, f32[4,18,40,1]{3,2,1,0:T(8,128)} %get-tuple-element.17, f32[4,18,40,383]{3,2,1,0:T(8,128)S(1)} %get-tuple-element.19, f32[4,18,40,383]{3,2,1,0:T(8,128)S(1)} %get-tuple-element.18, f32[4,18,40,1]{3,2,1,0:T(8,128)S(1)} %get-tuple-element.16, ...), kind=kLoop, calls=%fused_computation.9 | loop fusion | flops 8847360 | bytes 19906560 | tf_op jit(solution)/shard_map/add | solution.py:52
  24.1 3.3 %collective-permute-start.1 = (f32[4,18,1,384]{3,1,2,0:T(8,128)S(1)}, f32[4,18,1,384]{3,1,2,0:T(8,128)S(1)}, u32[]{:S(2)}, u32[]{:S(2)}) collective-permute-start(f32[4,18,1,384]{3,1,2,0:T(8,128)S(1)} %copy.26), channel_id=1, source_target_pairs={{8,0},{16,8},{24,16},{32,24},{40,32},{48,40},{56,48},{64,56},{72,6... | collective-permute-start | bytes 331784 | tf_op jit(solution)/shard_map/ppermute | solution.py:23
  27.5 4.1 %fusion.45 = (f32[4,18,39,384]{3,2,1,0:T(8,128)}, f32[4,18,39,384]{3,2,1,0:T(8,128)}) fusion(f32[4,18,40,384]{3,2,1,0:T(8,128)S(1)} %fusion.6), kind=kLoop, calls=%fused_computation.74 | loop fusion | bytes 17252352 | tf_op jit(solution)/shard_map/slice | solution.py:61
  32.4 2.2 collective-permute-done.2
  37.0 5.9 %fusion.10 = f32[4,18,40,384]{3,2,1,0:T(8,128)S(1)} fusion(f32[4,18,40,384]{3,2,1,0:T(8,128)} %copy-done.2, f32[4,18,1,384]{3,2,1,0:T(1,128)S(1)} %broadcast_select_fusion.3, f32[4,18,39,384]{3,2,1,0:T(8,128)} %get-tuple-element.15, f32[4,18,39,384]{3,2,1,0:T(8,128)} %get-tuple-element.14, f32[4,18,1,384]{3,2,1,0:T(1,128)S(1)} %broadcast_select_fusion.1, ...), kind=kLoop, calls=%fused_computation.15 | loop fusion | flops 8847360 | bytes 19906560 | tf_op jit(solution)/shard_map/add | solution.py:62
  42.9 1.5 collective-permute-start.3
  44.7 5.8 %collective-permute-done.3 = f32[4,1,40,384]{3,2,1,0:T(8,128)S(1)} collective-permute-done((f32[4,1,40,384]{3,2,1,0:T(8,128)S(1)}, f32[4,1,40,384]{3,2,1,0:T(8,128)S(1)}, u32[]{:S(2)}, u32[]{:S(2)}) %collective-permute-start.3) | collective-permute-done | bytes 245792 | tf_op jit(solution)/shard_map/ppermute | solution.py:12
  51.7 1.4 fusion.43
  53.1 3.5 %fusion.16 = f32[4,18,40,384]{3,2,1,0:T(8,128)S(1)} fusion(f32[4,18,40,384]{3,2,1,0:T(8,128)S(1)} %fusion.13, f32[4,18,40,1]{3,2,1,0:T(8,128)S(1)} %get-tuple-element.9, f32[4,18,40,383]{3,2,1,0:T(8,128)S(1)} %get-tuple-element.11, f32[4,18,40,383]{3,2,1,0:T(8,128)S(1)} %get-tuple-element.10, f32[4,18,40,1]{3,2,1,0:T(8,128)S(1)} %get-tuple-element.8, ...), kind=kLoop, calls=%fused_computation.24 | loop fusion | flops 8847360 | bytes 19906560 | tf_op jit(solution)/shard_map/add | solution.py:52
  56.8 9.9 %collective-permute-start.4 = (f32[4,18,1,384]{3,1,2,0:T(8,128)S(1)}, f32[4,18,1,384]{3,1,2,0:T(8,128)S(1)}, u32[]{:S(2)}, u32[]{:S(2)}) collective-permute-start(f32[4,18,1,384]{3,1,2,0:T(8,128)S(1)} %copy.32), channel_id=1, source_target_pairs={{8,0},{16,8},{24,16},{32,24},{40,32},{48,40},{56,48},{64,56},{72,6... | collective-permute-start | bytes 331784 | tf_op jit(solution)/shard_map/ppermute | solution.py:23
  66.8 4.1 %fusion.41 = (f32[4,18,39,384]{3,2,1,0:T(8,128)}, f32[4,18,39,384]{3,2,1,0:T(8,128)}) fusion(f32[4,18,40,384]{3,2,1,0:T(8,128)S(1)} %fusion.16), kind=kLoop, calls=%fused_computation.70 | loop fusion | bytes 17252352 | tf_op jit(solution)/shard_map/slice | solution.py:61
  74.2 5.7 %fusion.20 = f32[4,18,40,384]{3,2,1,0:T(8,128)S(1)} fusion(f32[4,18,40,384]{3,2,1,0:T(8,128)} %copy-done.1, f32[4,18,1,384]{3,2,1,0:T(1,128)S(1)} %broadcast_select_fusion.2, f32[4,18,39,384]{3,2,1,0:T(8,128)} %get-tuple-element.7, f32[4,18,39,384]{3,2,1,0:T(8,128)} %get-tuple-element.6, f32[4,18,1,384]{3,2,1,0:T(1,128)S(1)} %broadcast_select_fusion, ...), kind=kLoop, calls=%fused_computation.30 | loop fusion | flops 8847360 | bytes 19906560 | tf_op jit(solution)/shard_map/add | solution.py:62
  79.9 2.1 copy-done.3
  82.0 4.4 %fusion = f32[1,4,40,384]{3,0,2,1:T(1,128)S(1)} fusion(f32[4,18,40,384]{3,2,1,0:T(8,128)S(1)} %fusion.20, f32[18]{0:T(128)S(1)} %copy-done), kind=kOutput, calls=%fused_computation.1 | convolution fusion | flops 13271040 | bytes 4669512 | tf_op jit(solution)/shard_map/sxy,l,slxy->xy/dot_general | solution.py:89
  86.5 27.3 %psum.7 = f32[32,1,480]{2,1,0:T(1,128)} all-reduce(f32[32,1,480]{2,1,0:T(1,128)S(1)} %all_to_all.6), channel_id=1, replica_groups=mesh['tile'=32,'lev'=4,'sec'=2] {'lev','sec'}, use_global_device_ids=true, to_apply=%region_0.1 | all-reduce | flops 15360 | bytes 122880 | tf_op jit(solution)/shard_map/psum | solution.py:93
  113.9 14.8 %all-to-all-start = ((f32[32,1,480]{2,1,0:T(1,128)}), f32[32,1,480]{2,1,0:T(1,128)S(1)}, u32[]{:S(2)}, u32[]{:S(2)}) async-start(f32[32,1,480]{2,1,0:T(1,128)} %psum.7), calls=%async_computation | async-start | bytes 131072 | tf_op jit(solution)/shard_map/all_to_all | solution.py:94
  128.8 9.9 %all-to-all-done = f32[32,1,480]{2,1,0:T(1,128)S(1)} async-done(((f32[32,1,480]{2,1,0:T(1,128)}), f32[32,1,480]{2,1,0:T(1,128)S(1)}, u32[]{:S(2)}, u32[]{:S(2)}) %all-to-all-start) | async-done | bytes 61472 | tf_op jit(solution)/shard_map/all_to_all | solution.py:94
  139.0 81.0 %scatter_custom_fusion = f32[15360]{0:T(1024)} fusion(s32[15360]{0:T(1024)S(1)} %reshape.33, f32[15360]{0:T(1024)S(1)} %reshape.35, f32[]{:T(128)} %constant.16.clone.1), kind=kCustom, calls=%fused_computation.65 | custom fusion | flops 15360 | bytes 61444 | tf_op jit(solution)/shard_map/scatter-add | solution.py:95
  (65 shorter events, 11.8 us)
Async XLA Ops:
  0.6 81.3 %copy-start = (f32[18]{0:T(128)S(1)}, f32[18]{0:T(128)}, u32[]{:S(2)}) copy-start(f32[18]{0:T(128)} %param.15) | copy-start | bytes 220
  0.6 8.3 %slice-start = ((s8[4423680]{0:T(1024)(128)(4,1)}), s8[4194304]{0:T(1024)(128)(4,1)S(1)}, s32[]{:S(2)}) async-start(s8[4423680]{0:T(1024)(128)(4,1)} %bitcast.17), calls=%async_computation.1 | async-start | bytes 8388608
  1.8 7.2 %slice-start.1 = ((s8[4423680]{0:T(1024)(128)(4,1)}), s8[229376]{0:T(1024)(128)(4,1)S(1)}, s32[]{:S(2)}) async-start(s8[4423680]{0:T(1024)(128)(4,1)} %bitcast.17), calls=%async_computation.2 | async-start | bytes 458752
  1.8 10.2 %collective-permute-start = (f32[4,1,40,384]{3,2,1,0:T(8,128)S(1)}, f32[4,1,40,384]{3,2,1,0:T(8,128)S(1)}, u32[]{:S(2)}, u32[]{:S(2)}) collective-permute-start(f32[4,1,40,384]{3,2,1,0:T(8,128)S(1)} %slice.78), channel_id=1, source_target_pairs={{2,0},{4,2},{6,4},{3,1},{5,3},{7,5},{10,8},{12,10},{14,12},{11,9},... | collective-permute-start | bytes 737288 | tf_op jit(solution)/shard_map/ppermute | solution.py:12
  9.0 2.3 %copy-start.7 = (bf16[18,40,384]{2,1,0:T(8,128)(2,1)S(1)}, bf16[18,40,384]{2,1,0:T(8,128)(2,1)}, u32[]{:S(2)}) copy-start(bf16[18,40,384]{2,1,0:T(8,128)(2,1)} %param.12) | copy-start | bytes 1658884
  9.0 2.4 %copy-start.10 = (s32[32,2]{0,1:T(2,128)S(1)}, s32[32,2]{0,1:T(2,128)}, u32[]{:S(2)}) copy-start(s32[32,2]{0,1:T(2,128)} %param.14) | copy-start | bytes 772
  23.9 7.7 %copy-start.2 = (f32[4,18,40,384]{3,2,1,0:T(8,128)}, f32[4,18,40,384]{3,2,1,0:T(8,128)S(1)}, u32[]{:S(2)}) copy-start(f32[4,18,40,384]{3,2,1,0:T(8,128)S(1)} %fusion.6) | copy-start | bytes 13271044
  24.1 7.5 %collective-permute-start.1 = (f32[4,18,1,384]{3,1,2,0:T(8,128)S(1)}, f32[4,18,1,384]{3,1,2,0:T(8,128)S(1)}, u32[]{:S(2)}, u32[]{:S(2)}) collective-permute-start(f32[4,18,1,384]{3,1,2,0:T(8,128)S(1)} %copy.26), channel_id=1, source_target_pairs={{8,0},{16,8},{24,16},{32,24},{40,32},{48,40},{56,48},{64,56},{72,6... | collective-permute-start | bytes 331784 | tf_op jit(solution)/shard_map/ppermute | solution.py:23
  27.4 9.6 %copy-start.6 = (f32[18,40,384]{2,1,0:T(8,128)S(1)}, f32[18,40,384]{2,1,0:T(8,128)}, u32[]{:S(2)}) copy-start(f32[18,40,384]{2,1,0:T(8,128)} %get-tuple-element.22) | copy-start | bytes 3317764
  27.4 7.1 %collective-permute-start.2 = (f32[4,18,1,384]{3,1,2,0:T(8,128)S(1)}, f32[4,18,1,384]{3,1,2,0:T(8,128)S(1)}, u32[]{:S(2)}, u32[]{:S(2)}) collective-permute-start(f32[4,18,1,384]{3,1,2,0:T(8,128)S(1)} %copy.29), channel_id=1, source_target_pairs={{0,8},{8,16},{16,24},{24,32},{32,40},{40,48},{48,56},{56,64},{64,7... | collective-permute-start | bytes 331784 | tf_op jit(solution)/shard_map/ppermute | solution.py:22
  42.9 7.6 %collective-permute-start.3 = (f32[4,1,40,384]{3,2,1,0:T(8,128)S(1)}, f32[4,1,40,384]{3,2,1,0:T(8,128)S(1)}, u32[]{:S(2)}, u32[]{:S(2)}) collective-permute-start(f32[4,1,40,384]{3,2,1,0:T(8,128)S(1)} %slice.110), channel_id=1, source_target_pairs={{2,0},{4,2},{6,4},{3,1},{5,3},{7,5},{10,8},{12,10},{14,12},{11,9},... | collective-permute-start | bytes 737288 | tf_op jit(solution)/shard_map/ppermute | solution.py:12
  56.6 14.3 %copy-start.1 = (f32[4,18,40,384]{3,2,1,0:T(8,128)}, f32[4,18,40,384]{3,2,1,0:T(8,128)S(1)}, u32[]{:S(2)}) copy-start(f32[4,18,40,384]{3,2,1,0:T(8,128)S(1)} %fusion.16) | copy-start | bytes 13271044
  56.8 14.1 %collective-permute-start.4 = (f32[4,18,1,384]{3,1,2,0:T(8,128)S(1)}, f32[4,18,1,384]{3,1,2,0:T(8,128)S(1)}, u32[]{:S(2)}, u32[]{:S(2)}) collective-permute-start(f32[4,18,1,384]{3,1,2,0:T(8,128)S(1)} %copy.32), channel_id=1, source_target_pairs={{8,0},{16,8},{24,16},{32,24},{40,32},{48,40},{56,48},{64,56},{72,6... | collective-permute-start | bytes 331784 | tf_op jit(solution)/shard_map/ppermute | solution.py:23
  66.7 7.4 %copy-start.4 = (f32[18,40,384]{2,1,0:T(8,128)S(1)}, f32[18,40,384]{2,1,0:T(8,128)}, u32[]{:S(2)}) copy-start(f32[18,40,384]{2,1,0:T(8,128)} %get-tuple-element.20) | copy-start | bytes 3317764
  66.7 7.4 %copy-start.5 = (f32[18,40,384]{2,1,0:T(8,128)S(1)}, f32[18,40,384]{2,1,0:T(8,128)}, u32[]{:S(2)}) copy-start(f32[18,40,384]{2,1,0:T(8,128)} %get-tuple-element.21) | copy-start | bytes 3317764
  66.7 5.0 %collective-permute-start.5 = (f32[4,18,1,384]{3,1,2,0:T(8,128)S(1)}, f32[4,18,1,384]{3,1,2,0:T(8,128)S(1)}, u32[]{:S(2)}, u32[]{:S(2)}) collective-permute-start(f32[4,18,1,384]{3,1,2,0:T(8,128)S(1)} %copy.35), channel_id=1, source_target_pairs={{0,8},{8,16},{16,24},{24,32},{32,40},{40,48},{48,56},{56,64},{64,7... | collective-permute-start | bytes 331784 | tf_op jit(solution)/shard_map/ppermute | solution.py:22
  79.9 2.1 copy-start.3
  82.0 4.4 %copy-start.8 = (f32[4,40,384]{2,1,0:T(8,128)S(1)}, f32[4,40,384]{2,1,0:T(8,128)}, u32[]{:S(2)}) copy-start(f32[4,40,384]{2,1,0:T(8,128)} %param.16) | copy-start | bytes 737284
  82.0 46.7 %copy-start.9 = (s32[32,480]{1,0:T(8,128)S(1)}, s32[32,480]{1,0:T(8,128)}, u32[]{:S(2)}) copy-start(s32[32,480]{1,0:T(8,128)} %param.17) | copy-start | bytes 184324
  113.9 24.8 %all-to-all-start = ((f32[32,1,480]{2,1,0:T(1,128)}), f32[32,1,480]{2,1,0:T(1,128)S(1)}, u32[]{:S(2)}, u32[]{:S(2)}) async-start(f32[32,1,480]{2,1,0:T(1,128)} %psum.7), calls=%async_computation | async-start | bytes 131072 | tf_op jit(solution)/shard_map/all_to_all | solution.py:94
where the time goes:
time: 220 us
  other arithmetic  115 us (52%)
  starting transfers between devices  31.1 us (14%)
  blocking collectives  27.3 us (12%)
  local copies, waits for them, and re-layouts  23.3 us (11%)
  waiting for transfers between devices  17.9 us (8%)
  matrix products  4.36 us (2%)
    scatter-add x1, other arithmetic, shards(): jax.ops.segment_sum(received.reshape(-1), flux_cell.reshape(-1), num_segm...  81 us
    psum x1, blocking collectives, shards(): totals = lax.psum(columns, ('lev', 'sec'))  27.3 us
    all_to_all x1, starting transfers between devices, shards(): lax.all_to_all(totals, 'tile', split_axis=0, concat_axis=0, tiled=True)  14.8 us
    ppermute x2, starting transfers between devices, extended_2(): after = lax.ppermute(initial, axis, down)  13.2 us
    add x2, other arithmetic, sweep_first(): adjoint + ahead * (following - adjoint) + behind * (adjoint - previous)  11.6 us
    all_to_all x1, waiting for transfers between devices, shards(): lax.all_to_all(totals, 'tile', split_axis=0, concat_axis=0, tiled=True)  9.88 us
    slice x2, local copies, waits for them, and re-layouts, sweep_first(): previous = jnp.concatenate([left_rim, adjoint[:, :, :-1]], axis=2)  8.13 us
    add x2, other arithmetic, sweep_second(): adjoint + ahead * (following - adjoint) + behind * (adjoint - previous)  7.2 us
  transfers between devices with their start and end apart: 7, of which 3 were waited for; matrix products, arithmetic and copies ran while one was open for 9% of the time, Pallas kernels for 0%

commit v1 on v0

v1 whole, which is shorter than its diff:
```python
import functools

import jax
import jax.numpy as jnp
from jax import lax
from jax.experimental import pallas as pl
from jax.experimental.pallas import tpu as pltpu
from jax.sharding import PartitionSpec as P

SEC, LEV, ROWS, COLS = 4, 18, 40, 384
TILES = 32
OWNED = 15360
MESH = pl.DeviceIdType.MESH
ANY = pl.BlockSpec(memory_space=pl.ANY)
VMEM = pl.BlockSpec(memory_space=pltpu.VMEM)
SMEM = pl.BlockSpec(memory_space=pltpu.SMEM)
LIMIT = 56 * 1024 * 1024


def coefficients(courant, code, bit):
    size = jnp.abs(courant)
    rest = 1.0 - size
    twice = jnp.where((code & (1 << bit)) != 0, size * rest, 0.0)
    spread = 0.5 * twice
    positive = jnp.maximum(courant, 0.0)
    ahead = positive - spread
    back = (size - positive) - spread
    return ahead, back


def second_coefficients(courant, code, bit):
    ahead, back = coefficients(courant, code, bit)
    lane = lax.broadcasted_iota(jnp.int32, ahead.shape, 1)
    ahead = jnp.where(lane == COLS - 1, 0.0, ahead)
    back = jnp.where(lane == 0, 0.0, back)
    return ahead, back, 1.0 - ahead - back


def rims(left, right, flag_left, flag_right):
    both = jnp.concatenate([left, right], axis=0)
    lane = lax.broadcasted_iota(jnp.int32, (2 * SEC, 128), 1)
    parts = [
        jnp.take_along_axis(both[:, i * 128 : (i + 1) * 128], 127 - lane, axis=1)
        for i in (2, 1, 0)
    ]
    row = lax.broadcasted_iota(jnp.int32, both.shape, 0)
    flag = jnp.where(row < SEC, flag_left, flag_right)
    return jnp.where(flag == 1, jnp.concatenate(parts, axis=1), both)


def first_sweep(blocks, edges, sector, coefs):
    sub = lax.broadcasted_iota(jnp.int32, (8, COLS), 0)
    low = jnp.broadcast_to(edges[sector : sector + 1], (8, COLS))
    high = jnp.broadcast_to(edges[SEC + sector : SEC + sector + 1], (8, COLS))
    down = [low] + [pltpu.roll(b, 1, 0) for b in blocks]
    up = [pltpu.roll(b, 7, 0) for b in blocks] + [high]
    out = []
    for i, block in enumerate(blocks):
        ahead, back, centre = coefs[i]
        previous = jnp.where(sub == 0, down[i], down[i + 1])
        following = jnp.where(sub == 7, up[i + 1], up[i])
        out.append(centre * block + ahead * following + back * previous)
    return out


def first_coefficients(courant, code, bit):
    ahead, back = coefficients(courant.astype(jnp.float32), code, bit)
    centre = 1.0 - ahead - back
    return [
        (ahead[i : i + 8], back[i : i + 8], centre[i : i + 8]) for i in range(0, ROWS, 8)
    ]


def sweeps_kernel(
    seam,
    forcing,
    courant_x,
    courant_y,
    mass_flux,
    limiter,
    field,
    left0,
    right0,
    cx,
    cy,
    mf,
    code,
    halo1,
    halo0,
    passed,
    first1,
    last1,
    left1,
    right1,
    first0,
    last0,
    load_sem,
    lev_send,
    lev_recv,
    edge_send,
    edge_recv,
):
    tile, lev = lax.axis_index("tile"), lax.axis_index("lev")
    after, before = lax.rem(tile + 1, TILES), lax.rem(tile + TILES - 1, TILES)
    upper, lower = lax.rem(lev + 1, 4), lax.rem(lev + 3, 4)

    barrier = pltpu.get_barrier_semaphore()
    for device in ({"tile": after}, {"tile": before}, {"lev": upper}, {"lev": lower}):
        pl.semaphore_signal(barrier, inc=1, device_id=device, device_id_type=MESH)

    def loads(k):
        return (
            pltpu.make_async_copy(forcing.at[:, k], field.at[:, k], load_sem.at[0, k]),
            pltpu.make_async_copy(mass_flux.at[k], mf.at[k], load_sem.at[1, k]),
            pltpu.make_async_copy(courant_y.at[k], cy.at[k], load_sem.at[2, k]),
            pltpu.make_async_copy(limiter.at[k], code.at[k], load_sem.at[3, k]),
            pltpu.make_async_copy(courant_x.at[k], cx.at[k], load_sem.at[4, k]),
        )

    def start_loads(k, _):
        for copy in loads(k):
            copy.start()
        return 0

    lax.fori_loop(0, LEV, start_loads, 0)
    pl.semaphore_wait(barrier, 4)

    def level_copy(source, halo, index):
        return pltpu.make_async_remote_copy(
            source, halo, lev_send.at[index], lev_recv.at[index],
            device_id={"lev": lower}, device_id_type=MESH,
        )

    def edge_copies(k, step, first, last, left, right):
        return (
            pltpu.make_async_remote_copy(
                first.at[k], right.at[k], edge_send.at[step, 0, k], edge_recv.at[step, 0, k],
                device_id={"tile": before}, device_id_type=MESH,
            ),
            pltpu.make_async_remote_copy(
                last.at[k], left.at[k], edge_send.at[step, 1, k], edge_recv.at[step, 1, k],
                device_id={"tile": after}, device_id_type=MESH,
            ),
        )

    copy1 = level_copy(forcing.at[:, 0], halo1, 1)
    copy0 = level_copy(passed, halo0, 0)

    @pl.when(lev > 0)
    def _():
        copy1.start()

    def vertical_second(k, above, bit, step, first, last, left, right):
        for low, size in ((0, 16), (16, 16), (32, 8)):
            rows = slice(low, low + size)
            mixing = mf[k, rows, :].astype(jnp.float32)
            ahead, back, centre = second_coefficients(
                cy[k, rows, :].astype(jnp.float32), code[k, rows, :], bit
            )
            for s in range(SEC):
                value = field[s, k, rows, :]
                value = value + mixing * (above(s, rows) - value)
                value = (
                    centre * value
                    + ahead * pltpu.roll(value, COLS - 1, 1)
                    + back * pltpu.roll(value, 1, 1)
                )
                field[s, k, rows, :] = value
                if low == 0:
                    first[k, s : s + 1, :] = value[:1]
                if low == 32:
                    last[k, s : s + 1, :] = value[7:]
        for copy in edge_copies(k, step, first, last, left, right):
            copy.start()

    step1 = (3, 1, first1, last1, left1, right1)
    step0 = (1, 0, first0, last0, left0, right0)

    loads(0)[0].wait()

    def phase_a(k, _):
        loads(k + 1)[0].wait()
        for copy in loads(k)[1:4]:
            copy.wait()
        vertical_second(k, lambda s, rows: field[s, k + 1, rows, :], *step1)
        return 0

    lax.fori_loop(0, LEV - 1, phase_a, 0)

    def fill(halo, copy):
        @pl.when(lev < 3)
        def _():
            copy.wait_recv()

        @pl.when(lev == 3)
        def _():
            for s in range(SEC):
                halo[s] = field[s, LEV - 1]

    flag_left, flag_right = seam[tile, 0], seam[tile, 1]

    def phase_b(k, _):
        @pl.when(k == 9)
        def _():
            for copy in loads(LEV - 1)[1:4]:
                copy.wait()
            fill(halo1, copy1)
            vertical_second(LEV - 1, lambda s, rows: halo1[s, rows, :], *step1)

        loads(k)[4].wait()
        for copy in edge_copies(k, 1, first1, last1, left1, right1):
            copy.wait_recv()
        edges = rims(left1[k], right1[k], flag_left, flag_right)
        coefs = first_coefficients(cx[k], code[k], 2)
        for s in range(SEC):
            blocks = [field[s, k, i : i + 8, :] for i in range(0, ROWS, 8)]
            for i, block in enumerate(first_sweep(blocks, edges, s, coefs)):
                field[s, k, i * 8 : i * 8 + 8, :] = block

        @pl.when(k == 0)
        def _():
            for s in range(SEC):
                passed[s] = field[s, 0]

        @pl.when(jnp.logical_and(k == 0, lev > 0))
        def _():
            copy0.start()

        @pl.when(k > 0)
        def _():
            vertical_second(k - 1, lambda s, rows: field[s, k, rows, :], *step0)

        return 0

    lax.fori_loop(0, LEV, phase_b, 0)
    fill(halo0, copy0)
    vertical_second(LEV - 1, lambda s, rows: halo0[s, rows, :], *step0)

    def finish(k, _):
        for copy in edge_copies(k, 1, first1, last1, left1, right1):
            copy.wait_send()
        for copy in edge_copies(k, 0, first0, last0, left0, right0):
            copy.wait()
        return 0

    lax.fori_loop(0, LEV, finish, 0)

    @pl.when(lev > 0)
    def _():
        copy1.wait_send()
        copy0.wait_send()


def last_kernel(seam, weight, field, courant_x, limiter, left, right, share, out, partial, total):
    k = pl.program_id(0)
    tile = lax.axis_index("tile")
    edges = rims(left[0], right[0], seam[tile, 0], seam[tile, 1])
    coefs = first_coefficients(courant_x[0], limiter[0], 0)

    @pl.when(k == 0)
    def _():
        total[...] = jnp.zeros_like(total)

    sums = None
    for s in range(SEC):
        blocks = [field[s, 0, i : i + 8, :] for i in range(0, ROWS, 8)]
        results = first_sweep(blocks, edges, s, coefs)
        terms = []
        for i, block in enumerate(results):
            rows = slice(i * 8, i * 8 + 8)
            out[s, 0, rows, :] = block
            terms.append(share[s, rows, :] * block)
        sums = terms if sums is None else [a + b for a, b in zip(sums, terms)]
    for i, term in enumerate(sums):
        rows = slice(i * 8, i * 8 + 8)
        total[rows, :] += weight[k] * term

    @pl.when(k == LEV - 1)
    def _():
        for q in range(8):
            partial[q] = total[5 * q : 5 * q + 5, :]


def remap_kernel(
    partial, cells, out, others, outgoing, arrived, high, low,
    rs_send, rs_recv, send_sem, recv_sem,
):
    tile, lev, sec = lax.axis_index("tile"), lax.axis_index("lev"), lax.axis_index("sec")
    me = lev * 2 + sec
    mine = tile // 4

    barrier = pltpu.get_barrier_semaphore()
    own = mine == me

    def member(q):
        return {"tile": tile, "lev": q // 2, "sec": lax.rem(q, 2)}

    for p in range(1, 8):
        pl.semaphore_signal(
            barrier, inc=1, device_id=member(lax.rem(me + p, 8)), device_id_type=MESH
        )

    def greet(t, _):
        @pl.when(jnp.logical_not(jnp.logical_and(own, t == tile)))
        def _():
            pl.semaphore_signal(
                barrier, inc=1,
                device_id={"tile": t, "lev": mine // 2, "sec": lax.rem(mine, 2)},
                device_id_type=MESH,
            )
        return 0

    lax.fori_loop(0, TILES, greet, 0)

    @pl.when(own)
    def _():
        pl.semaphore_wait(barrier, 7 + 31)

    @pl.when(jnp.logical_not(own))
    def _():
        pl.semaphore_wait(barrier, 7 + 32)

    def reduce_copy(p):
        peer = lax.rem(me + p, 8)
        return pltpu.make_async_remote_copy(
            partial.at[peer], others.at[p - 1], rs_send.at[p - 1], rs_recv.at[p - 1],
            device_id=member(peer), device_id_type=MESH,
        )

    for p in range(1, 8):
        reduce_copy(p).start()

    slot = lax.broadcasted_iota(jnp.int32, (128, 512), 0)

    def one_hot(t, _):
        cell = cells[t]
        high[t] = jnp.where(slot == (cell >> 7), 1.0, 0.0).astype(jnp.bfloat16)
        low[t] = jnp.where(slot == (cell & 127), 1.0, 0.0).astype(jnp.bfloat16)
        return 0

    lax.fori_loop(0, TILES, one_hot, 0)

    summed = partial[me]
    for p in range(1, 8):
        reduce_copy(p).wait_recv()
        summed = summed + others[p - 1]
    for r in range(4):
        pair = jnp.concatenate([summed[r : r + 1], summed[r + 1 : r + 2]], axis=1)
        if r:
            pair = pltpu.roll(pair, 768 - 96 * r, 1)
        outgoing[r] = pair[:, :512]

    def send_copy(i):
        owner = me * 4 + i // 8
        return pltpu.make_async_remote_copy(
            outgoing.at[i // 8], arrived.at[tile], send_sem.at[i], recv_sem.at[tile],
            device_id={"tile": owner, "lev": lax.rem(i, 8) // 2, "sec": lax.rem(i, 2)},
            device_id_type=MESH,
        )

    def is_self(i):
        return jnp.logical_and(me * 4 + i // 8 == tile, lax.rem(i, 8) == me)

    def send(i, _):
        @pl.when(jnp.logical_not(is_self(i)))
        def _():
            send_copy(i).start()

        @pl.when(is_self(i))
        def _():
            pltpu.make_async_copy(
                outgoing.at[i // 8], arrived.at[tile], recv_sem.at[tile]
            ).start()
        return 0

    lax.fori_loop(0, TILES, send, 0)

    def accumulate(t, total):
        pltpu.make_async_copy(arrived.at[t], arrived.at[t], recv_sem.at[t]).wait()
        value = arrived[t]
        for _ in range(3):
            piece = value.astype(jnp.bfloat16)
            value = value - piece.astype(jnp.float32)
            spread = high[t] * jnp.broadcast_to(piece, (128, 512))
            total = total + lax.dot_general(
                spread, low[t], (((1,), (1,)), ((), ())),
                preferred_element_type=jnp.float32,
            )
        return total

    total = lax.fori_loop(0, TILES, accumulate, jnp.zeros((128, 128), jnp.float32))
    out[...] = total[: OWNED // 128]

    for p in range(1, 8):
        reduce_copy(p).wait_send()

    def finish(i, _):
        @pl.when(jnp.logical_not(is_self(i)))
        def _():
            send_copy(i).wait_send()
        return 0

    lax.fori_loop(0, TILES, finish, 0)


def shards(
    forcing, courant_x, courant_y, mass_flux, limiter_code, seam_code, level_weight,
    sector_share, flux_cell,
):
    f32, bf16, i32 = jnp.float32, jnp.bfloat16, jnp.int32
    shape = jax.ShapeDtypeStruct
    dma = pltpu.SemaphoreType.DMA
    edge = (LEV, SEC, COLS)
    plane = (SEC, ROWS, COLS)
    grid3 = (LEV, ROWS, COLS)
    field, left0, right0 = pl.pallas_call(
        sweeps_kernel,
        out_shape=(shape(forcing.shape, f32), shape(edge, f32), shape(edge, f32)),
        in_specs=[SMEM] + [ANY] * 5,
        out_specs=[VMEM] * 3,
        scratch_shapes=[
            pltpu.VMEM(grid3, bf16),
            pltpu.VMEM(grid3, bf16),
            pltpu.VMEM(grid3, bf16),
            pltpu.VMEM(grid3, i32),
            pltpu.VMEM(plane, f32),
            pltpu.VMEM(plane, f32),
            pltpu.VMEM(plane, f32),
        ]
        + [pltpu.VMEM(edge, f32)] * 6
        + [dma((5, LEV)), dma((2,)), dma((2,)), dma((2, 2, LEV)), dma((2, 2, LEV))],
        compiler_params=pltpu.CompilerParams(
            collective_id=0, has_side_effects=True, vmem_limit_bytes=LIMIT
        ),
        name="sweeps",
    )(seam_code, forcing, courant_x, courant_y, mass_flux, limiter_code)

    level = pl.BlockSpec((SEC, 1, ROWS, COLS), lambda k: (0, k, 0, 0))
    one = pl.BlockSpec((1, ROWS, COLS), lambda k: (k, 0, 0))
    rim = pl.BlockSpec((1, SEC, COLS), lambda k: (k, 0, 0))
    adjoint, partial = pl.pallas_call(
        last_kernel,
        out_shape=(shape(forcing.shape, f32), shape((8, 5, COLS), f32)),
        grid=(LEV,),
        in_specs=[
            SMEM, SMEM, level, one, one, rim, rim,
            pl.BlockSpec((SEC, ROWS, COLS), lambda k: (0, 0, 0)),
        ],
        out_specs=[level, pl.BlockSpec((8, 5, COLS), lambda k: (0, 0, 0))],
        scratch_shapes=[pltpu.VMEM((ROWS, COLS), f32)],
        compiler_params=pltpu.CompilerParams(vmem_limit_bytes=LIMIT),
        name="last_sweep",
    )(seam_code, level_weight, field, courant_x, limiter_code, left0, right0, sector_share)

    cells = jnp.pad(flux_cell, ((0, 0), (0, 32)), constant_values=-1)[:, None, :]
    flux = pl.pallas_call(
        remap_kernel,
        out_shape=shape((OWNED // 128, 128), f32),
        in_specs=[VMEM, VMEM],
        out_specs=VMEM,
        scratch_shapes=[
            pltpu.VMEM((7, 5, COLS), f32),
            pltpu.VMEM((4, 1, 512), f32),
            pltpu.VMEM((TILES, 1, 512), f32),
            pltpu.VMEM((TILES, 128, 512), bf16),
            pltpu.VMEM((TILES, 128, 512), bf16),
            dma((7,)), dma((7,)), dma((TILES,)), dma((TILES,)),
        ],
        compiler_params=pltpu.CompilerParams(
            collective_id=1, has_side_effects=True, vmem_limit_bytes=LIMIT
        ),
        name="remap",
    )(partial, cells)
    return adjoint, flux.reshape(-1)


def solution(mesh):
    placed = (
        P("sec", "lev", "tile", None),
        P("lev", "tile", None),
        P("lev", "tile", None),
        P("lev", "tile", None),
        P("lev", "tile", None),
        P(),
        P("lev"),
        P("sec", "tile", None),
        P("tile", None),
    )
    return jax.shard_map(
        shards,
        mesh=mesh,
        in_specs=placed,
        out_specs=(P("sec", "lev", "tile", None), P("tile")),
        check_vma=False,
    )
```

time: 220 us -> 84.3 us (0.38)
  other arithmetic: 115 us -> 0 us
  Pallas kernels: 0 us -> 79.6 us
  starting transfers between devices: 31.1 us -> 0 us
  blocking collectives: 27.3 us -> 0 us
  local copies, waits for them, and re-layouts: 23.3 us -> 3.51 us
  waiting for transfers between devices: 17.9 us -> 0 us
  matrix products: 4.36 us -> 0 us
    scatter-add x1 -> x0, other arithmetic: 81 us -> none  [shards(): jax.ops.segment_sum(received.reshape(-1), flux_cell.reshape(-1), num_segm...]
    pallas_call x0 -> x3, Pallas kernels: none -> 79.6 us  [the longest x1 40 us: shards(): pl.pallas_call(sweeps_kernel, out_shape=(shape(forcing.shape, f32), shape...]
    psum x1 -> x0, blocking collectives: 27.3 us -> none  [shards(): totals = lax.psum(columns, ('lev', 'sec'))]
    add x6 -> x0, other arithmetic: 23.7 us -> none  [the longest x2 11.6 us: sweep_first(): adjoint + ahead * (following - adjoint) + behind * (adjoint - previous)]
    slice x17 -> x0, local copies, waits for them, and re-layouts: 17.6 us -> none  [the longest x2 8.13 us: sweep_first(): previous = jnp.concatenate([left_rim, adjoint[:, :, :-1]], axis=2)]
    ppermute x6 -> x0, starting transfers between devices: 16.3 us -> none  [the longest x2 13.2 us: extended_2(): after = lax.ppermute(initial, axis, down)]
    all_to_all x1 -> x0, starting transfers between devices: 14.8 us -> none  [shards(): lax.all_to_all(totals, 'tile', split_axis=0, concat_axis=0, tiled=True)]
    all_to_all x1 -> x0, waiting for transfers between devices: 9.88 us -> none  [shards(): lax.all_to_all(totals, 'tile', split_axis=0, concat_axis=0, tiled=True)]
  transfers between devices with their start and end apart: 7 -> 0, of which waited for: 3 -> 0; matrix products, arithmetic and copies ran while one was open for 9% -> 0% of each run, Pallas kernels for 0% -> 0%
where the time goes in v1:
time: 84.3 us; the launch traced here: 83.8 us
  Pallas kernels  79.6 us (94%)
  local copies, waits for them, and re-layouts  3.51 us (4%)
    pallas_call x1, Pallas kernels, shards(): pl.pallas_call(sweeps_kernel, out_shape=(shape(forcing.shape, f32), shape...  40 us
    pallas_call x1, Pallas kernels, shards(): pl.pallas_call(remap_kernel, out_shape=shape((OWNED // 128, 128), f32), i...  26.5 us
    pallas_call x1, Pallas kernels, shards(): pl.pallas_call(last_kernel, out_shape=(shape(forcing.shape, f32), shape((...  13.1 us
    unnamed x4, local copies, waits for them, and re-layouts  2.83 us

profile of v1, /device:TPU:1, one launch (start us, length us, event | category | flops | bytes accessed | tf_op | source)
XLA Modules:
  0.0 83.8 jit_solution(7772364905850802654)
XLA Ops:
  0.6 1.4 %copy.12.seam = s32[32,2]{1,0:T(8,128)} copy(s32[32,2]{0,1:T(2,128)} %param.14) | data formatting | bytes 512 | tf_op args[5]
  2.0 40.0 %sweeps.1 = (f32[4,18,40,384]{3,2,1,0:T(8,128)}, f32[18,4,384]{2,1,0:T(4,128)}, f32[18,4,384]{2,1,0:T(4,128)}) custom-call(s32[32,2]{1,0:T(8,128)} %copy.12.seam, f32[4,18,40,384]{3,2,1,0:T(8,128)} %forcing.1, bf16[18,40,384]{2,1,0:T(8,128)(2,1)} %courant_x.3, bf16[18,40,384]{2,1,0:T(8,128)(2,1)} %courant_y.1, bf16[18,40,384]{2,1,0:T(8,128)(2,1)} %mass_flux.1, ...), custom_call_target="tpu_custom_call" | custom-call | tf_op jit(solution)/shard_map/sweeps/pallas_call | solution.py:416
  42.0 0.0 copy-start
  42.0 13.1 %last_sweep.1 = (f32[4,18,40,384]{3,2,1,0:T(8,128)}, f32[8,5,384]{2,1,0:T(8,128)}) custom-call(s32[32,2]{1,0:T(8,128)} %copy.12.seam, f32[18]{0:T(128)} %weight.1, f32[4,18,40,384]{3,2,1,0:T(8,128)} %get-tuple-element.7.field, bf16[18,40,384]{2,1,0:T(8,128)(2,1)} %courant_x.3, s32[18,40,384]{2,1,0:T(8,128)} %limiter.3, f32[18,4,384]{2,1,0:T(4,128)} %get-tuple-element.8.left, ...), custom_call_target="tpu_custom_call" | custom-call | tf_op jit(solution)/shard_map/last_sweep/pallas_call | solution.py:441
  55.1 0.0 copy-done
  55.1 0.7 broadcast_in_dim.3.cells
  55.8 26.5 %remap.1 = f32[120,128]{1,0:T(8,128)} custom-call(f32[8,5,384]{2,1,0:T(8,128)} %get-tuple-element.11.partial, s32[32,1,512]{2,1,0:T(1,128)} %broadcast_in_dim.3.cells), custom_call_target="tpu_custom_call" | custom-call | tf_op jit(solution)/shard_map/remap/pallas_call | solution.py:456
  82.3 1.5 %copy.14 = f32[15360]{0:T(1024)} copy(f32[15360]{0:T(1024)} %bitcast.1) | data formatting | bytes 122880
  (1 shorter events, 0.0 us)
Async XLA Ops:
  42.0 13.1 %copy-start = (s32[32,480]{1,0:T(8,128)S(1)}, s32[32,480]{1,0:T(8,128)}, u32[]{:S(2)}) copy-start(s32[32,480]{1,0:T(8,128)} %param.17) | copy-start | bytes 184324

commit v2 on v1

v2 whole, which is shorter than its diff:
```python
import functools

import jax
import jax.numpy as jnp
from jax import lax
from jax.experimental import pallas as pl
from jax.experimental.pallas import tpu as pltpu
from jax.sharding import PartitionSpec as P

SEC, LEV, ROWS, COLS = 4, 18, 40, 384
TILES = 32
OWNED = 15360
MESH = pl.DeviceIdType.MESH
HBM = pl.BlockSpec(memory_space=pltpu.HBM)
VMEM = pl.BlockSpec(memory_space=pltpu.VMEM)
SMEM = pl.BlockSpec(memory_space=pltpu.SMEM)
MIB = 1024 * 1024
LIMIT_FIRST = 32
LIMIT_SECOND = 18


def coefficients(courant, code, bit):
    size = jnp.abs(courant)
    rest = 1.0 - size
    twice = jnp.where((code & (1 << bit)) != 0, size * rest, 0.0)
    spread = 0.5 * twice
    positive = jnp.maximum(courant, 0.0)
    ahead = positive - spread
    back = (size - positive) - spread
    return ahead, back


def second_coefficients(courant, code, bit):
    ahead, back = coefficients(courant, code, bit)
    lane = lax.broadcasted_iota(jnp.int32, ahead.shape, 1)
    ahead = jnp.where(lane == COLS - 1, 0.0, ahead)
    back = jnp.where(lane == 0, 0.0, back)
    return ahead, back, 1.0 - ahead - back


def rims(left, right, flag_left, flag_right):
    both = jnp.concatenate([left, right], axis=0)
    lane = lax.broadcasted_iota(jnp.int32, (2 * SEC, 128), 1)
    parts = [
        jnp.take_along_axis(both[:, i * 128 : (i + 1) * 128], 127 - lane, axis=1)
        for i in (2, 1, 0)
    ]
    row = lax.broadcasted_iota(jnp.int32, both.shape, 0)
    flag = jnp.where(row < SEC, flag_left, flag_right)
    return jnp.where(flag == 1, jnp.concatenate(parts, axis=1), both)


def first_sweep(blocks, edges, sector, coefs):
    sub = lax.broadcasted_iota(jnp.int32, (8, COLS), 0)
    low = jnp.broadcast_to(edges[sector : sector + 1], (8, COLS))
    high = jnp.broadcast_to(edges[SEC + sector : SEC + sector + 1], (8, COLS))
    down = [low] + [pltpu.roll(b, 1, 0) for b in blocks]
    up = [pltpu.roll(b, 7, 0) for b in blocks] + [high]
    out = []
    for i, block in enumerate(blocks):
        ahead, back, centre = coefs[i]
        previous = jnp.where(sub == 0, down[i], down[i + 1])
        following = jnp.where(sub == 7, up[i + 1], up[i])
        out.append(centre * block + ahead * following + back * previous)
    return out


def first_coefficients(courant, code, bit):
    ahead, back = coefficients(courant.astype(jnp.float32), code, bit)
    centre = 1.0 - ahead - back
    return [
        (ahead[i : i + 8], back[i : i + 8], centre[i : i + 8]) for i in range(0, ROWS, 8)
    ]


def adjoint_kernel(
    seam_code,
    level_weight,
    forcing,
    courant_x,
    courant_y,
    mass_flux,
    limiter,
    sector_share,
    flux_cell,
    out,
    arrived,
    high,
    low,
    seam,
    weight,
    field,
    swept,
    cx,
    cy,
    mf,
    code,
    share,
    cells,
    padded,
    halo1,
    halo0,
    first1,
    last1,
    left1,
    right1,
    first0,
    last0,
    left0,
    right0,
    total,
    partial,
    others,
    outgoing,
    load_sem,
    extra_sem,
    lev_send,
    lev_recv,
    edge_send,
    edge_recv,
    rs_send,
    rs_recv,
    send_sem,
    recv_sem,
):
    tile, lev, sec = lax.axis_index("tile"), lax.axis_index("lev"), lax.axis_index("sec")
    after, before = lax.rem(tile + 1, TILES), lax.rem(tile + TILES - 1, TILES)
    upper, lower = lax.rem(lev + 1, 4), lax.rem(lev + 3, 4)
    me = lev * 2 + sec
    mine = tile // 4
    own = mine == me

    def member(q):
        return {"tile": tile, "lev": q // 2, "sec": lax.rem(q, 2)}

    def loads(k):
        return (
            pltpu.make_async_copy(forcing.at[:, k], field.at[:, k], load_sem.at[0, k]),
            pltpu.make_async_copy(mass_flux.at[k], mf.at[k], load_sem.at[1, k]),
            pltpu.make_async_copy(courant_y.at[k], cy.at[k], load_sem.at[2, k]),
            pltpu.make_async_copy(limiter.at[k], code.at[k], load_sem.at[3, k]),
            pltpu.make_async_copy(courant_x.at[k], cx.at[k], load_sem.at[4, k]),
        )

    def start_loads(k, _):
        for copy in loads(k):
            copy.start()
        return 0

    share_copy = pltpu.make_async_copy(sector_share, share, extra_sem.at[0])
    cells_copy = pltpu.make_async_copy(flux_cell, cells, extra_sem.at[1])
    seam_copy = pltpu.make_async_copy(seam_code, seam, extra_sem.at[2])
    weight_copy = pltpu.make_async_copy(level_weight, weight, extra_sem.at[3])

    barrier = pltpu.get_barrier_semaphore()
    for device in ({"tile": after}, {"tile": before}, {"lev": upper}, {"lev": lower}):
        pl.semaphore_signal(barrier, inc=1, device_id=device, device_id_type=MESH)
    for p in range(1, 8):
        pl.semaphore_signal(
            barrier, inc=1, device_id=member(lax.rem(me + p, 8)), device_id_type=MESH
        )

    def greet(t, _):
        @pl.when(jnp.logical_not(jnp.logical_and(own, t == tile)))
        def _():
            pl.semaphore_signal(
                barrier, inc=1,
                device_id={"tile": t, "lev": mine // 2, "sec": lax.rem(mine, 2)},
                device_id_type=MESH,
            )
        return 0

    lax.fori_loop(0, TILES, greet, 0)
    lax.fori_loop(0, LEV, start_loads, 0)
    for copy in (share_copy, cells_copy, seam_copy, weight_copy):
        copy.start()

    @pl.when(own)
    def _():
        pl.semaphore_wait(barrier, 4 + 7 + 31)

    @pl.when(jnp.logical_not(own))
    def _():
        pl.semaphore_wait(barrier, 4 + 7 + 32)

    def level_copy(source, halo, index):
        return pltpu.make_async_remote_copy(
            source, halo, lev_send.at[index], lev_recv.at[index],
            device_id={"lev": lower}, device_id_type=MESH,
        )

    def edge_copies(k, step, first, last, left, right):
        return (
            pltpu.make_async_remote_copy(
                first.at[k], right.at[k], edge_send.at[step, 0, k], edge_recv.at[step, 0, k],
                device_id={"tile": before}, device_id_type=MESH,
            ),
            pltpu.make_async_remote_copy(
                last.at[k], left.at[k], edge_send.at[step, 1, k], edge_recv.at[step, 1, k],
                device_id={"tile": after}, device_id_type=MESH,
            ),
        )

    copy1 = level_copy(forcing.at[:, 0], halo1, 1)
    copy0 = level_copy(field.at[:, 0], halo0, 0)

    @pl.when(lev > 0)
    def _():
        copy1.start()

    def vertical_second(k, above, bit, step, first, last, left, right):
        for start, size in ((0, 16), (16, 16), (32, 8)):
            rows = slice(start, start + size)
            mixing = mf[k, rows, :].astype(jnp.float32)
            ahead, back, centre = second_coefficients(
                cy[k, rows, :].astype(jnp.float32), code[k, rows, :], bit
            )
            for s in range(SEC):
                value = field[s, k, rows, :]
                value = value + mixing * (above(s, rows) - value)
                value = (
                    centre * value
                    + ahead * pltpu.roll(value, COLS - 1, 1)
                    + back * pltpu.roll(value, 1, 1)
                )
                swept[s, k, rows, :] = value
                if start == 0:
                    first[k, s : s + 1, :] = value[:1]
                if start == 32:
                    last[k, s : s + 1, :] = value[7:]
        for copy in edge_copies(k, step, first, last, left, right):
            copy.start()

    edges1 = (first1, last1, left1, right1)
    edges0 = (first0, last0, left0, right0)
    step1 = (3, 1) + edges1
    step0 = (1, 0) + edges0

    loads(0)[0].wait()

    def phase_a(k, _):
        loads(k + 1)[0].wait()
        for copy in loads(k)[1:4]:
            copy.wait()
        vertical_second(k, lambda s, rows: field[s, k + 1, rows, :], *step1)
        return 0

    lax.fori_loop(0, LEV - 1, phase_a, 0)

    def fill(halo, copy):
        @pl.when(lev < 3)
        def _():
            copy.wait_recv()

        @pl.when(lev == 3)
        def _():
            for s in range(SEC):
                halo[s] = field[s, LEV - 1]

    seam_copy.wait()
    flag_left, flag_right = seam[0, tile], seam[1, tile]

    def first_dimension(k, step, edges, bit, target):
        for copy in edge_copies(k, step, *edges):
            copy.wait_recv()
        rim = rims(edges[2][k], edges[3][k], flag_left, flag_right)
        coefs = first_coefficients(cx[k], code[k], bit)
        results = []
        for s in range(SEC):
            blocks = [swept[s, k, i : i + 8, :] for i in range(0, ROWS, 8)]
            blocks = first_sweep(blocks, rim, s, coefs)
            for i, block in enumerate(blocks):
                target[s, k, i * 8 : i * 8 + 8, :] = block
            results.append(blocks)
        return results

    loads(0)[4].wait()
    first_dimension(0, 1, edges1, 2, field)

    @pl.when(lev > 0)
    def _():
        copy0.start()

    def phase_b(k, _):
        @pl.when(k == 8)
        def _():
            for copy in loads(LEV - 1)[1:4]:
                copy.wait()
            fill(halo1, copy1)
            vertical_second(LEV - 1, lambda s, rows: halo1[s, rows, :], *step1)

        loads(k + 1)[4].wait()
        first_dimension(k + 1, 1, edges1, 2, field)
        vertical_second(k, lambda s, rows: field[s, k + 1, rows, :], *step0)
        return 0

    lax.fori_loop(0, LEV - 1, phase_b, 0)

    share_copy.wait()
    weight_copy.wait()
    total[...] = jnp.zeros_like(total)

    def phase_c(k, _):
        @pl.when(k == 8)
        def _():
            fill(halo0, copy0)
            vertical_second(LEV - 1, lambda s, rows: halo0[s, rows, :], *step0)

        results = first_dimension(k, 0, edges0, 0, out)
        for i in range(ROWS // 8):
            rows = slice(i * 8, i * 8 + 8)
            term = share[0, rows, :] * results[0][i]
            for s in range(1, SEC):
                term = term + share[s, rows, :] * results[s][i]
            total[rows, :] += weight[k] * term
        return 0

    lax.fori_loop(0, LEV, phase_c, 0)

    for q in range(8):
        partial[q] = total[5 * q : 5 * q + 5, :]

    def reduce_copy(p):
        return pltpu.make_async_remote_copy(
            partial.at[lax.rem(me + p, 8)], others.at[p - 1],
            rs_send.at[p - 1], rs_recv.at[p - 1],
            device_id=member(lax.rem(me + p, 8)), device_id_type=MESH,
        )

    for p in range(1, 8):
        reduce_copy(p).start()

    cells_copy.wait()
    padded[...] = jnp.concatenate(
        [cells[...], jnp.full((TILES, 32), -1, jnp.int32)], axis=1
    )
    slot = lax.broadcasted_iota(jnp.int32, (128, 512), 0)

    def one_hot(t, _):
        cell = padded[pl.ds(t, 1), :]
        high[t] = jnp.where(slot == (cell >> 7), 1.0, 0.0).astype(jnp.bfloat16)
        low[t] = jnp.where(slot == (cell & 127), 1.0, 0.0).astype(jnp.bfloat16)
        return 0

    lax.fori_loop(0, TILES, one_hot, 0)

    summed = partial[me]
    for p in range(1, 8):
        reduce_copy(p).wait_recv()
        summed = summed + others[p - 1]
    for r in range(4):
        pair = jnp.concatenate([summed[r : r + 1], summed[r + 1 : r + 2]], axis=1)
        if r:
            pair = pltpu.roll(pair, 768 - 96 * r, 1)
        outgoing[r] = pair[:, :512]

    def send_copy(i):
        return pltpu.make_async_remote_copy(
            outgoing.at[i // 8], arrived.at[tile], send_sem.at[i], recv_sem.at[tile],
            device_id={
                "tile": me * 4 + i // 8, "lev": lax.rem(i, 8) // 2, "sec": lax.rem(i, 2),
            },
            device_id_type=MESH,
        )

    def is_self(i):
        return jnp.logical_and(me * 4 + i // 8 == tile, lax.rem(i, 8) == me)

    def send(i, _):
        @pl.when(jnp.logical_not(is_self(i)))
        def _():
            send_copy(i).start()

        @pl.when(is_self(i))
        def _():
            pltpu.make_async_copy(
                outgoing.at[i // 8], arrived.at[tile], recv_sem.at[tile]
            ).start()
        return 0

    lax.fori_loop(0, TILES, send, 0)

    def finish_edges(k, _):
        for copy in edge_copies(k, 1, *edges1) + edge_copies(k, 0, *edges0):
            copy.wait_send()
        return 0

    lax.fori_loop(0, LEV, finish_edges, 0)

    @pl.when(lev > 0)
    def _():
        copy1.wait_send()
        copy0.wait_send()

    for p in range(1, 8):
        reduce_copy(p).wait_send()

    def finish(i, _):
        @pl.when(jnp.logical_not(is_self(i)))
        def _():
            send_copy(i).wait_send()

        pltpu.make_async_copy(arrived.at[i], arrived.at[i], recv_sem.at[i]).wait()
        return 0

    lax.fori_loop(0, TILES, finish, 0)


def remap_kernel(adjoint, arrived, high, low, adjoint_out, flux, sem):
    copy = pltpu.make_async_copy(adjoint, adjoint_out, sem)
    copy.start()

    def accumulate(t, total):
        value = arrived[t]
        for _ in range(3):
            piece = value.astype(jnp.bfloat16)
            value = value - piece.astype(jnp.float32)
            spread = high[t] * jnp.broadcast_to(piece, (128, 512))
            total = total + lax.dot_general(
                spread, low[t], (((1,), (1,)), ((), ())),
                preferred_element_type=jnp.float32,
            )
        return total

    total = lax.fori_loop(
        0, TILES, accumulate, jnp.zeros((128, 128), jnp.float32), unroll=4
    )
    flux[...] = total[: OWNED // 128]
    copy.wait()


def shards(
    forcing, courant_x, courant_y, mass_flux, limiter_code, seam_code, level_weight,
    sector_share, flux_cell,
):
    f32, bf16, i32 = jnp.float32, jnp.bfloat16, jnp.int32
    shape = jax.ShapeDtypeStruct
    dma = pltpu.SemaphoreType.DMA
    edge = pltpu.VMEM((LEV, SEC, COLS), f32)
    plane = pltpu.VMEM((SEC, ROWS, COLS), f32)
    levels = (LEV, ROWS, COLS)
    passed = pl.pallas_call(
        adjoint_kernel,
        out_shape=(
            shape(forcing.shape, f32),
            shape((TILES, 1, 512), f32),
            shape((TILES, 128, 512), bf16),
            shape((TILES, 128, 512), bf16),
        ),
        in_specs=[HBM] * 9,
        out_specs=[VMEM] * 4,
        scratch_shapes=[pltpu.SMEM((2, TILES), i32), pltpu.SMEM((LEV,), f32)]
        + [pltpu.VMEM(forcing.shape, f32)] * 2
        + [pltpu.VMEM(levels, bf16)] * 3
        + [pltpu.VMEM(levels, i32)]
        + [plane]
        + [pltpu.VMEM((TILES, 480), i32), pltpu.VMEM((TILES, 512), i32)]
        + [plane] * 2
        + [edge] * 8
        + [
            pltpu.VMEM((ROWS, COLS), f32),
            pltpu.VMEM((8, 5, COLS), f32),
            pltpu.VMEM((7, 5, COLS), f32),
            pltpu.VMEM((4, 1, 512), f32),
        ]
        + [dma((5, LEV)), dma((4,)), dma((2,)), dma((2,)), dma((2, 2, LEV)), dma((2, 2, LEV))]
        + [dma((7,)), dma((7,)), dma((TILES,)), dma((TILES,))],
        compiler_params=pltpu.CompilerParams(
            collective_id=0, has_side_effects=True, vmem_limit_bytes=LIMIT_FIRST * MIB
        ),
        name="adjoint",
    )(
        *(
            pltpu.with_memory_space_constraint(x, pltpu.HBM)
            for x in (
                seam_code.T, level_weight, forcing, courant_x, courant_y, mass_flux,
                limiter_code, sector_share, flux_cell,
            )
        ),
    )
    adjoint, flux = pl.pallas_call(
        remap_kernel,
        out_shape=(shape(forcing.shape, f32), shape((OWNED // 128, 128), f32)),
        in_specs=[VMEM] * 4,
        out_specs=[HBM, VMEM],
        scratch_shapes=[dma],
        compiler_params=pltpu.CompilerParams(vmem_limit_bytes=LIMIT_SECOND * MIB),
        name="remap",
    )(*passed)
    return adjoint, flux.reshape(-1)


def solution(mesh):
    placed = (
        P("sec", "lev", "tile", None),
        P("lev", "tile", None),
        P("lev", "tile", None),
        P("lev", "tile", None),
        P("lev", "tile", None),
        P(),
        P("lev"),
        P("sec", "tile", None),
        P("tile", None),
    )
    return jax.shard_map(
        shards,
        mesh=mesh,
        in_specs=placed,
        out_specs=(P("sec", "lev", "tile", None), P("tile")),
        check_vma=False,
    )
```

time: 84.3 us -> 49.1 us (0.58)
  Pallas kernels: 79.6 us -> 48.3 us
  local copies, waits for them, and re-layouts: 3.51 us -> 0 us
    pallas_call x3 -> x2, Pallas kernels: 79.6 us -> 48.3 us  [the longest x1 43.1 us: shards(): pl.pallas_call(adjoint_kernel, out_shape=(shape(forcing.shape, f32), shap...]
    unnamed x4 -> x0, local copies, waits for them, and re-layouts: 2.83 us -> none
where the time goes in v2:
time: 49.1 us; the launch traced here: 49 us
  Pallas kernels  48.3 us (98%)
  between operations  0.64 us (1%)
    pallas_call x1, Pallas kernels, shards(): pl.pallas_call(adjoint_kernel, out_shape=(shape(forcing.shape, f32), shap...  43.1 us
    pallas_call x1, Pallas kernels, shards(): pl.pallas_call(remap_kernel, out_shape=(shape(forcing.shape, f32), shape(...  5.25 us

profile of v2, /device:TPU:1, one launch (start us, length us, event | category | flops | bytes accessed | tf_op | source)
XLA Modules:
  0.0 49.0 jit_solution(1129244421620241353)
XLA Ops:
  0.6 43.1 %adjoint.1 = (f32[4,18,40,384]{3,2,1,0:T(8,128)S(1)}, f32[32,1,512]{2,1,0:T(1,128)S(1)}, bf16[32,128,512]{2,1,0:T(8,128)(2,1)S(1)}, bf16[32,128,512]{2,1,0:T(8,128)(2,1)S(1)}) custom-call(s32[2,32]{1,0:T(2,128)} %bitcast.2, f32[18]{0:T(128)} %level_weight.1, f32[4,18,40,384]{3,2,1,0:T(8,128)} %forcing.1, bf16[18,40,384]{2,1,0:T(8,128)(2,1)} %courant_x.1, ...), custom_call_target="tpu_custom_call" | custom-call | tf_op jit(solution)/shard_map/adjoint/pallas_call | solution.py:442
  43.7 5.3 %remap.1 = (f32[4,18,40,384]{3,2,1,0:T(8,128)}, f32[120,128]{1,0:T(8,128)}) custom-call(f32[4,18,40,384]{3,2,1,0:T(8,128)S(1)} %get-tuple-element.8.adjoint, f32[32,1,512]{2,1,0:T(1,128)S(1)} %get-tuple-element.9.arrived, bf16[32,128,512]{2,1,0:T(8,128)(2,1)S(1)} %get-tuple-element.10.high, bf16[32,128,512]{2,1,0:T(8,128)(2,1)S(1)} %get-tuple-element.11.low), custom_call_target="tpu_custom_call" | custom-call | tf_op jit(solution)/shard_map/remap/pallas_call | solution.py:481

commit v3 on v2

--- a/solution.py
+++ b/solution.py
@@ -15,8 +15,9 @@
 VMEM = pl.BlockSpec(memory_space=pltpu.VMEM)
 SMEM = pl.BlockSpec(memory_space=pltpu.SMEM)
 MIB = 1024 * 1024
-LIMIT_FIRST = 32
-LIMIT_SECOND = 18
+LIMIT_FIRST = 40
+LIMIT_SECOND = 8
+MEET_AT, HALO1_AT, TAIL_AT, HALO0_AT = 2, 12, 8, 14
 
 
 def coefficients(courant, code, bit):
@@ -84,9 +85,7 @@
     sector_share,
     flux_cell,
     out,
-    arrived,
-    high,
-    low,
+    flux,
     seam,
     weight,
     field,
@@ -112,6 +111,9 @@
     partial,
     others,
     outgoing,
+    arrived,
+    high,
+    low,
     load_sem,
     extra_sem,
     lev_send,
@@ -122,13 +124,12 @@
     rs_recv,
     send_sem,
     recv_sem,
+    ready,
 ):
     tile, lev, sec = lax.axis_index("tile"), lax.axis_index("lev"), lax.axis_index("sec")
     after, before = lax.rem(tile + 1, TILES), lax.rem(tile + TILES - 1, TILES)
-    upper, lower = lax.rem(lev + 1, 4), lax.rem(lev + 3, 4)
+    lower = lax.rem(lev + 3, 4)
     me = lev * 2 + sec
-    mine = tile // 4
-    own = mine == me
 
     def member(q):
         return {"tile": tile, "lev": q // 2, "sec": lax.rem(q, 2)}
@@ -153,35 +154,30 @@
     weight_copy = pltpu.make_async_copy(level_weight, weight, extra_sem.at[3])
 
     barrier = pltpu.get_barrier_semaphore()
-    for device in ({"tile": after}, {"tile": before}, {"lev": upper}, {"lev": lower}):
+    along_z, along_x, core = tile // 8, lax.rem(tile // 2, 4), lax.rem(tile, 2)
+
+    def tile_at(z, x, c):
+        return {"tile": (lax.rem(z, 4) * 4 + lax.rem(x, 4)) * 2 + lax.rem(c, 2)}
+
+    beside_z = [tile_at(along_z + i, along_x, core) for i in (1, 3)]
+    beside_x = [tile_at(along_z, along_x + i, core) for i in (1, 3)]
+    near = [{"tile": after}, {"tile": before}] + beside_z + beside_x
+    near += [member(lax.rem(me + p, 8)) for p in range(1, 8)]
+    for device in near:
         pl.semaphore_signal(barrier, inc=1, device_id=device, device_id_type=MESH)
-    for p in range(1, 8):
-        pl.semaphore_signal(
-            barrier, inc=1, device_id=member(lax.rem(me + p, 8)), device_id_type=MESH
-        )
-
-    def greet(t, _):
-        @pl.when(jnp.logical_not(jnp.logical_and(own, t == tile)))
-        def _():
-            pl.semaphore_signal(
-                barrier, inc=1,
-                device_id={"tile": t, "lev": mine // 2, "sec": lax.rem(mine, 2)},
-                device_id_type=MESH,
-            )
-        return 0
-
-    lax.fori_loop(0, TILES, greet, 0)
+
+    stages = (beside_z, beside_z, beside_x, beside_x, [tile_at(along_z, along_x, core + 1)])
+
+    def tell(i):
+        for device in stages[i]:
+            pl.semaphore_signal(ready.at[i], inc=1, device_id=device, device_id_type=MESH)
+
+    def hear(i):
+        pl.semaphore_wait(ready.at[i], len(stages[i]))
+
     lax.fori_loop(0, LEV, start_loads, 0)
     for copy in (share_copy, cells_copy, seam_copy, weight_copy):
         copy.start()
-
-    @pl.when(own)
-    def _():
-        pl.semaphore_wait(barrier, 4 + 7 + 31)
-
-    @pl.when(jnp.logical_not(own))
-    def _():
-        pl.semaphore_wait(barrier, 4 + 7 + 32)
 
     def level_copy(source, halo, index):
         return pltpu.make_async_remote_copy(
@@ -204,9 +200,13 @@
     copy1 = level_copy(forcing.at[:, 0], halo1, 1)
     copy0 = level_copy(field.at[:, 0], halo0, 0)
 
-    @pl.when(lev > 0)
-    def _():
-        copy1.start()
+    def meet():
+        pl.semaphore_wait(barrier, len(near))
+        tell(0)
+
+        @pl.when(lev > 0)
+        def _():
+            copy1.start()
 
     def vertical_second(k, above, bit, step, first, last, left, right):
         for start, size in ((0, 16), (16, 16), (32, 8)):
@@ -228,7 +228,9 @@
                     first[k, s : s + 1, :] = value[:1]
                 if start == 32:
                     last[k, s : s + 1, :] = value[7:]
-        for copy in edge_copies(k, step, first, last, left, right):
+
+    def send_edges(k, step, edges):
+        for copy in edge_copies(k, step, *edges):
             copy.start()
 
     edges1 = (first1, last1, left1, right1)
@@ -243,6 +245,21 @@
         for copy in loads(k)[1:4]:
             copy.wait()
         vertical_second(k, lambda s, rows: field[s, k + 1, rows, :], *step1)
+
+        @pl.when(k == MEET_AT)
+        def _():
+            meet()
+
+            def earlier(j, _):
+                send_edges(j, 1, edges1)
+                return 0
+
+            lax.fori_loop(0, MEET_AT, earlier, 0)
+
+        @pl.when(k >= MEET_AT)
+        def _():
+            send_edges(k, 1, edges1)
+
         return 0
 
     lax.fori_loop(0, LEV - 1, phase_a, 0)
@@ -281,30 +298,54 @@
     def _():
         copy0.start()
 
+    hear(0)
+    tell(1)
+
     def phase_b(k, _):
-        @pl.when(k == 8)
+        for stage, turn in ((1, 5), (2, 11)):
+
+            @pl.when(k == turn)
+            def _():
+                hear(stage)
+                tell(stage + 1)
+
+        @pl.when(k == HALO1_AT)
         def _():
             for copy in loads(LEV - 1)[1:4]:
                 copy.wait()
             fill(halo1, copy1)
             vertical_second(LEV - 1, lambda s, rows: halo1[s, rows, :], *step1)
+            send_edges(LEV - 1, 1, edges1)
 
         loads(k + 1)[4].wait()
         first_dimension(k + 1, 1, edges1, 2, field)
         vertical_second(k, lambda s, rows: field[s, k + 1, rows, :], *step0)
-        return 0
-
-    lax.fori_loop(0, LEV - 1, phase_b, 0)
-
+        send_edges(k, 0, edges0)
+        return 0
+
+    lax.fori_loop(0, LEV - 2, phase_b, 0)
+    loads(LEV - 1)[4].wait()
     share_copy.wait()
     weight_copy.wait()
     total[...] = jnp.zeros_like(total)
 
     def phase_c(k, _):
-        @pl.when(k == 8)
+        @pl.when(k == 2)
+        def _():
+            hear(3)
+            tell(4)
+
+        @pl.when(k == TAIL_AT)
+        def _():
+            first_dimension(LEV - 1, 1, edges1, 2, field)
+            vertical_second(LEV - 2, lambda s, rows: field[s, LEV - 1, rows, :], *step0)
+            send_edges(LEV - 2, 0, edges0)
+
+        @pl.when(k == HALO0_AT)
         def _():
             fill(halo0, copy0)
             vertical_second(LEV - 1, lambda s, rows: halo0[s, rows, :], *step0)
+            send_edges(LEV - 1, 0, edges0)
 
         results = first_dimension(k, 0, edges0, 0, out)
         for i in range(ROWS // 8):
@@ -378,7 +419,34 @@
             ).start()
         return 0
 
+    hear(4)
     lax.fori_loop(0, TILES, send, 0)
+
+    def step_of(a):
+        return a + a // 2 - 2 * (a // 3)
+
+    def accumulate(group, total):
+        sources = []
+        for j in range(4):
+            z = lax.rem(along_z + step_of(group // 2), 4)
+            x = lax.rem(along_x + step_of(2 * lax.rem(group, 2) + j // 2), 4)
+            sources.append((z * 4 + x) * 2 + lax.rem(core + j % 2, 2))
+        for t in sources:
+            pltpu.make_async_copy(arrived.at[t], arrived.at[t], recv_sem.at[t]).wait()
+        for t in sources:
+            value = arrived[t]
+            for _ in range(3):
+                piece = value.astype(jnp.bfloat16)
+                value = value - piece.astype(jnp.float32)
+                spread = high[t] * jnp.broadcast_to(piece, (128, 512))
+                total = total + lax.dot_general(
+                    spread, low[t], (((1,), (1,)), ((), ())),
+                    preferred_element_type=jnp.float32,
+                )
+        return total
+
+    sums = lax.fori_loop(0, TILES // 4, accumulate, jnp.zeros((128, 128), jnp.float32))
+    flux[...] = sums[: OWNED // 128]
 
     def finish_edges(k, _):
         for copy in edge_copies(k, 1, *edges1) + edge_copies(k, 0, *edges0):
@@ -399,34 +467,20 @@
         @pl.when(jnp.logical_not(is_self(i)))
         def _():
             send_copy(i).wait_send()
-
-        pltpu.make_async_copy(arrived.at[i], arrived.at[i], recv_sem.at[i]).wait()
         return 0
 
     lax.fori_loop(0, TILES, finish, 0)
 
 
-def remap_kernel(adjoint, arrived, high, low, adjoint_out, flux, sem):
-    copy = pltpu.make_async_copy(adjoint, adjoint_out, sem)
-    copy.start()
-
-    def accumulate(t, total):
-        value = arrived[t]
-        for _ in range(3):
-            piece = value.astype(jnp.bfloat16)
-            value = value - piece.astype(jnp.float32)
-            spread = high[t] * jnp.broadcast_to(piece, (128, 512))
-            total = total + lax.dot_general(
-                spread, low[t], (((1,), (1,)), ((), ())),
-                preferred_element_type=jnp.float32,
-            )
-        return total
-
-    total = lax.fori_loop(
-        0, TILES, accumulate, jnp.zeros((128, 128), jnp.float32), unroll=4
+def store_kernel(adjoint, flux, adjoint_out, flux_out, sem):
+    copies = (
+        pltpu.make_async_copy(adjoint, adjoint_out, sem.at[0]),
+        pltpu.make_async_copy(flux, flux_out, sem.at[1]),
     )
-    flux[...] = total[: OWNED // 128]
-    copy.wait()
+    for copy in copies:
+        copy.start()
+    for copy in copies:
+        copy.wait()
 
 
 def shards(
@@ -443,12 +497,10 @@
         adjoint_kernel,
         out_shape=(
             shape(forcing.shape, f32),
-            shape((TILES, 1, 512), f32),
-            shape((TILES, 128, 512), bf16),
-            shape((TILES, 128, 512), bf16),
+            shape((OWNED // 128, 128), f32),
         ),
         in_specs=[HBM] * 9,
-        out_specs=[VMEM] * 4,
+        out_specs=[VMEM] * 2,
         scratch_shapes=[pltpu.SMEM((2, TILES), i32), pltpu.SMEM((LEV,), f32)]
         + [pltpu.VMEM(forcing.shape, f32)] * 2
         + [pltpu.VMEM(levels, bf16)] * 3
@@ -462,9 +514,13 @@
             pltpu.VMEM((8, 5, COLS), f32),
             pltpu.VMEM((7, 5, COLS), f32),
             pltpu.VMEM((4, 1, 512), f32),
+            pltpu.VMEM((TILES, 1, 512), f32),
+            pltpu.VMEM((TILES, 128, 512), bf16),
+            pltpu.VMEM((TILES, 128, 512), bf16),
         ]
         + [dma((5, LEV)), dma((4,)), dma((2,)), dma((2,)), dma((2, 2, LEV)), dma((2, 2, LEV))]
-        + [dma((7,)), dma((7,)), dma((TILES,)), dma((TILES,))],
+        + [dma((7,)), dma((7,)), dma((TILES,)), dma((TILES,))]
+        + [pltpu.SemaphoreType.REGULAR((5,))],
         compiler_params=pltpu.CompilerParams(
             collective_id=0, has_side_effects=True, vmem_limit_bytes=LIMIT_FIRST * MIB
         ),
@@ -479,13 +535,13 @@
         ),
     )
     adjoint, flux = pl.pallas_call(
-        remap_kernel,
+        store_kernel,
         out_shape=(shape(forcing.shape, f32), shape((OWNED // 128, 128), f32)),
-        in_specs=[VMEM] * 4,
-        out_specs=[HBM, VMEM],
-        scratch_shapes=[dma],
+        in_specs=[VMEM] * 2,
+        out_specs=[HBM] * 2,
+        scratch_shapes=[dma((2,))],
         compiler_params=pltpu.CompilerParams(vmem_limit_bytes=LIMIT_SECOND * MIB),
-        name="remap",
+        name="store",
     )(*passed)
     return adjoint, flux.reshape(-1)
 

time: 49.1 us -> 46.7 us (0.951)
  the two profiles are of different devices: /device:TPU:1 before, /device:TPU:7 now
where the time goes in v3:
time: 46.7 us
  Pallas kernels  46 us (99%)
  between operations  0.64 us (1%)
    pallas_call x1, Pallas kernels, shards(): pl.pallas_call(adjoint_kernel, out_shape=(shape(forcing.shape, f32), shap...  43.9 us
    pallas_call x1, Pallas kernels, shards(): pl.pallas_call(store_kernel, out_shape=(shape(forcing.shape, f32), shape(...  2.11 us

profile of v3, /device:TPU:7, one launch (start us, length us, event | category | flops | bytes accessed | tf_op | source)
XLA Modules:
  0.0 46.7 jit_solution(7513563111715677613)
XLA Ops:
  0.6 43.9 %adjoint.1 = (f32[4,18,40,384]{3,2,1,0:T(8,128)S(1)}, f32[120,128]{1,0:T(8,128)S(1)}) custom-call(s32[2,32]{1,0:T(2,128)} %bitcast.2, f32[18]{0:T(128)} %level_weight.1, f32[4,18,40,384]{3,2,1,0:T(8,128)} %forcing.1, bf16[18,40,384]{2,1,0:T(8,128)(2,1)} %courant_x.1, bf16[18,40,384]{2,1,0:T(8,128)(2,1)} %courant_y.1, bf16[18,40,384]{2,1,0:T(8,128)(2,1)} %mass_flux.1, ...), custom_call_target="tpu_custom_call" | custom-call | tf_op jit(solution)/shard_map/adjoint/pallas_call | solution.py:496
  44.5 2.1 %store.1 = (f32[4,18,40,384]{3,2,1,0:T(8,128)}, f32[120,128]{1,0:T(8,128)}) custom-call(f32[4,18,40,384]{3,2,1,0:T(8,128)S(1)} %get-tuple-element.6.adjoint, f32[120,128]{1,0:T(8,128)S(1)} %get-tuple-element.7.flux), custom_call_target="tpu_custom_call" | custom-call | tf_op jit(solution)/shard_map/store/pallas_call | solution.py:537

commit v4 on v3

--- a/solution.py
+++ b/solution.py
@@ -17,7 +17,9 @@
 MIB = 1024 * 1024
 LIMIT_FIRST = 40
 LIMIT_SECOND = 8
-MEET_AT, HALO1_AT, TAIL_AT, HALO0_AT = 2, 12, 8, 14
+CHUNKS = ((0, 16), (16, 16), (32, 8))
+PARTS = ((0, 8), (32, 8), (8, 24))
+EDGE1_AT, EDGE0_AT, REST0_AT = 0, 0, 2
 
 
 def coefficients(courant, code, bit):
@@ -134,18 +136,23 @@
     def member(q):
         return {"tile": tile, "lev": q // 2, "sec": lax.rem(q, 2)}
 
-    def loads(k):
+    def loads(i):
+        pair = pl.ds(2 * i, 2)
         return (
-            pltpu.make_async_copy(forcing.at[:, k], field.at[:, k], load_sem.at[0, k]),
-            pltpu.make_async_copy(mass_flux.at[k], mf.at[k], load_sem.at[1, k]),
-            pltpu.make_async_copy(courant_y.at[k], cy.at[k], load_sem.at[2, k]),
-            pltpu.make_async_copy(limiter.at[k], code.at[k], load_sem.at[3, k]),
-            pltpu.make_async_copy(courant_x.at[k], cx.at[k], load_sem.at[4, k]),
+            pltpu.make_async_copy(forcing.at[:, pair], field.at[:, pair], load_sem.at[0, i]),
+            pltpu.make_async_copy(mass_flux.at[pair], mf.at[pair], load_sem.at[1, i]),
+            pltpu.make_async_copy(courant_y.at[pair], cy.at[pair], load_sem.at[2, i]),
+            pltpu.make_async_copy(limiter.at[pair], code.at[pair], load_sem.at[3, i]),
+            pltpu.make_async_copy(courant_x.at[pair], cx.at[pair], load_sem.at[4, i]),
         )
 
-    def start_loads(k, _):
-        for copy in loads(k):
+    def start_loads(i, _):
+        for copy in loads(i)[:4]:
             copy.start()
+        return 0
+
+    def start_late_loads(i, _):
+        loads(i)[4].start()
         return 0
 
     share_copy = pltpu.make_async_copy(sector_share, share, extra_sem.at[0])
@@ -175,41 +182,53 @@
     def hear(i):
         pl.semaphore_wait(ready.at[i], len(stages[i]))
 
-    lax.fori_loop(0, LEV, start_loads, 0)
+    lax.fori_loop(0, LEV // 2, start_loads, 0)
+    lax.fori_loop(0, LEV // 2, start_late_loads, 0)
     for copy in (share_copy, cells_copy, seam_copy, weight_copy):
         copy.start()
 
-    def level_copy(source, halo, index):
-        return pltpu.make_async_remote_copy(
-            source, halo, lev_send.at[index], lev_recv.at[index],
-            device_id={"lev": lower}, device_id_type=MESH,
-        )
-
-    def edge_copies(k, step, first, last, left, right):
+    def level_copies(source, halo, step):
+        return [
+            pltpu.make_async_remote_copy(
+                source.at[:, 0, pl.ds(start, size)], halo.at[:, pl.ds(start, size)],
+                lev_send.at[step, i], lev_recv.at[step, i],
+                device_id={"lev": lower}, device_id_type=MESH,
+            )
+            for i, (start, size) in enumerate(PARTS)
+        ]
+
+    def edge_copies(group, step, first, last, left, right):
+        if isinstance(group, int) and group >= 4:
+            part = pl.ds(12 + group, 1)
+        else:
+            part = pl.ds(4 * group, 4)
         return (
             pltpu.make_async_remote_copy(
-                first.at[k], right.at[k], edge_send.at[step, 0, k], edge_recv.at[step, 0, k],
+                first.at[part], right.at[part],
+                edge_send.at[step, 0, group], edge_recv.at[step, 0, group],
                 device_id={"tile": before}, device_id_type=MESH,
             ),
             pltpu.make_async_remote_copy(
-                last.at[k], left.at[k], edge_send.at[step, 1, k], edge_recv.at[step, 1, k],
+                last.at[part], left.at[part],
+                edge_send.at[step, 1, group], edge_recv.at[step, 1, group],
                 device_id={"tile": after}, device_id_type=MESH,
             ),
         )
 
-    copy1 = level_copy(forcing.at[:, 0], halo1, 1)
-    copy0 = level_copy(field.at[:, 0], halo0, 0)
+    def start_levels(source, halo, step):
+        @pl.when(lev > 0)
+        def _():
+            for copy in level_copies(source, halo, step):
+                copy.start()
 
     def meet():
         pl.semaphore_wait(barrier, len(near))
         tell(0)
 
-        @pl.when(lev > 0)
-        def _():
-            copy1.start()
-
-    def vertical_second(k, above, bit, step, first, last, left, right):
-        for start, size in ((0, 16), (16, 16), (32, 8)):
+        start_levels(forcing, halo1, 1)
+
+    def vertical_second(k, above, bit, step, first, last, left, right, chunks=CHUNKS):
+        for start, size in chunks:
             rows = slice(start, start + size)
             mixing = mf[k, rows, :].astype(jnp.float32)
             ahead, back, centre = second_coefficients(
@@ -229,57 +248,83 @@
                 if start == 32:
                     last[k, s : s + 1, :] = value[7:]
 
-    def send_edges(k, step, edges):
-        for copy in edge_copies(k, step, *edges):
+    def send_edges(group, step, edges):
+        for copy in edge_copies(group, step, *edges):
             copy.start()
+
+    def take_edges(group, step, edges):
+        for copy in edge_copies(group, step, *edges):
+            copy.wait_recv()
 
     edges1 = (first1, last1, left1, right1)
     edges0 = (first0, last0, left0, right0)
     step1 = (3, 1) + edges1
     step0 = (1, 0) + edges0
 
+    def inner_level(k, step_args):
+        vertical_second(k, lambda s, rows: field[s, k + 1, rows, :], *step_args)
+
     loads(0)[0].wait()
 
-    def phase_a(k, _):
-        loads(k + 1)[0].wait()
-        for copy in loads(k)[1:4]:
-            copy.wait()
-        vertical_second(k, lambda s, rows: field[s, k + 1, rows, :], *step1)
-
-        @pl.when(k == MEET_AT)
+    def phase_a(g, _):
+        for i in range(2):
+            for copy in loads(2 * g + i)[1:4]:
+                copy.wait()
+            loads(2 * g + i + 1)[0].wait()
+        for j in range(4):
+            inner_level(4 * g + j, step1)
+
+        @pl.when(g == 0)
         def _():
             meet()
 
-            def earlier(j, _):
-                send_edges(j, 1, edges1)
-                return 0
-
-            lax.fori_loop(0, MEET_AT, earlier, 0)
-
-        @pl.when(k >= MEET_AT)
-        def _():
-            send_edges(k, 1, edges1)
-
-        return 0
-
-    lax.fori_loop(0, LEV - 1, phase_a, 0)
-
-    def fill(halo, copy):
+        send_edges(g, 1, edges1)
+        return 0
+
+    lax.fori_loop(0, 4, phase_a, 0)
+    for copy in loads(8)[1:4]:
+        copy.wait()
+    inner_level(16, step1)
+    send_edges(4, 1, edges1)
+
+    def top_level(source, halo, step, step_args, parts):
+        copies = level_copies(source, halo, step)
+
         @pl.when(lev < 3)
         def _():
-            copy.wait_recv()
+            for i in parts:
+                copies[i].wait_recv()
 
         @pl.when(lev == 3)
         def _():
-            for s in range(SEC):
-                halo[s] = field[s, LEV - 1]
+            for i in parts:
+                start, size = PARTS[i]
+                for s in range(SEC):
+                    halo[s, start : start + size] = field[s, LEV - 1, start : start + size]
+
+        vertical_second(
+            LEV - 1, lambda s, rows: halo[s, rows, :], *step_args,
+            chunks=[PARTS[i] for i in parts],
+        )
+
+    cells_copy.wait()
+    padded[...] = jnp.concatenate(
+        [cells[...], jnp.full((TILES, 32), -1, jnp.int32)], axis=1
+    )
+    slot = lax.broadcasted_iota(jnp.int32, (128, 512), 0)
+
+    def one_hot(t, _):
+        cell = padded[pl.ds(t, 1), :]
+        high[t] = jnp.where(slot == (cell >> 7), 1.0, 0.0).astype(jnp.bfloat16)
+        low[t] = jnp.where(slot == (cell & 127), 1.0, 0.0).astype(jnp.bfloat16)
+        return 0
+
+    lax.fori_loop(0, TILES, one_hot, 0)
 
     seam_copy.wait()
     flag_left, flag_right = seam[0, tile], seam[1, tile]
 
-    def first_dimension(k, step, edges, bit, target):
-        for copy in edge_copies(k, step, *edges):
-            copy.wait_recv()
+    def first_dimension(k, edges, bit, target):
         rim = rims(edges[2][k], edges[3][k], flag_left, flag_right)
         coefs = first_coefficients(cx[k], code[k], bit)
         results = []
@@ -291,72 +336,97 @@
             results.append(blocks)
         return results
 
-    loads(0)[4].wait()
-    first_dimension(0, 1, edges1, 2, field)
-
-    @pl.when(lev > 0)
-    def _():
-        copy0.start()
-
     hear(0)
     tell(1)
 
-    def phase_b(k, _):
-        for stage, turn in ((1, 5), (2, 11)):
-
-            @pl.when(k == turn)
-            def _():
-                hear(stage)
-                tell(stage + 1)
-
-        @pl.when(k == HALO1_AT)
-        def _():
-            for copy in loads(LEV - 1)[1:4]:
-                copy.wait()
-            fill(halo1, copy1)
-            vertical_second(LEV - 1, lambda s, rows: halo1[s, rows, :], *step1)
-            send_edges(LEV - 1, 1, edges1)
-
-        loads(k + 1)[4].wait()
-        first_dimension(k + 1, 1, edges1, 2, field)
-        vertical_second(k, lambda s, rows: field[s, k + 1, rows, :], *step0)
-        send_edges(k, 0, edges0)
-        return 0
-
-    lax.fori_loop(0, LEV - 2, phase_b, 0)
-    loads(LEV - 1)[4].wait()
+    def first_group(g):
+        take_edges(g, 1, edges1)
+        for i in range(2):
+            loads(2 * g + i)[4].wait()
+        for j in range(4):
+            first_dimension(4 * g + j, edges1, 2, field)
+
+    def second_group(g):
+        for j in range(4):
+            inner_level(4 * g + j, step0)
+        send_edges(g, 0, edges0)
+
+    def early_top1():
+        top_level(forcing, halo1, 1, step1, (0, 1))
+        send_edges(5, 1, edges1)
+
+    def early_top0():
+        take_edges(5, 1, edges1)
+        first_dimension(17, edges1, 2, field)
+        inner_level(16, step0)
+        send_edges(4, 0, edges0)
+        top_level(field, halo0, 0, step0, (0, 1))
+        send_edges(5, 0, edges0)
+
+    first_group(0)
+    start_levels(field, halo0, 0)
+
+    def phase_b(g, _):
+        first_group(g + 1)
+        second_group(g)
+
+        @pl.when(g == EDGE1_AT)
+        def _():
+            early_top1()
+
+        @pl.when(g == 1)
+        def _():
+            hear(1)
+            tell(2)
+
+        return 0
+
+    lax.fori_loop(0, 3, phase_b, 0)
+    take_edges(4, 1, edges1)
+    loads(8)[4].wait()
+    first_dimension(16, edges1, 2, field)
+    second_group(3)
+    hear(2)
+    tell(3)
+    top_level(forcing, halo1, 1, step1, (2,))
+
     share_copy.wait()
     weight_copy.wait()
     total[...] = jnp.zeros_like(total)
 
-    def phase_c(k, _):
-        @pl.when(k == 2)
-        def _():
-            hear(3)
-            tell(4)
-
-        @pl.when(k == TAIL_AT)
-        def _():
-            first_dimension(LEV - 1, 1, edges1, 2, field)
-            vertical_second(LEV - 2, lambda s, rows: field[s, LEV - 1, rows, :], *step0)
-            send_edges(LEV - 2, 0, edges0)
-
-        @pl.when(k == HALO0_AT)
-        def _():
-            fill(halo0, copy0)
-            vertical_second(LEV - 1, lambda s, rows: halo0[s, rows, :], *step0)
-            send_edges(LEV - 1, 0, edges0)
-
-        results = first_dimension(k, 0, edges0, 0, out)
+    def last_level(k):
+        results = first_dimension(k, edges0, 0, out)
         for i in range(ROWS // 8):
             rows = slice(i * 8, i * 8 + 8)
             term = share[0, rows, :] * results[0][i]
             for s in range(1, SEC):
                 term = term + share[s, rows, :] * results[s][i]
             total[rows, :] += weight[k] * term
-        return 0
-
-    lax.fori_loop(0, LEV, phase_c, 0)
+
+    def phase_c(g, _):
+        @pl.when(g == EDGE0_AT)
+        def _():
+            early_top0()
+
+        @pl.when(g == REST0_AT)
+        def _():
+            top_level(field, halo0, 0, step0, (2,))
+
+        @pl.when(g == 1)
+        def _():
+            hear(3)
+            tell(4)
+
+        take_edges(g, 0, edges0)
+        for j in range(4):
+            last_level(4 * g + j)
+        return 0
+
+    lax.fori_loop(0, 4, phase_c, 0)
+    take_edges(4, 0, edges0)
+    last_level(16)
+    take_edges(5, 0, edges0)
+    last_level(17)
 
     for q in range(8):
         partial[q] = total[5 * q : 5 * q + 5, :]
@@ -370,20 +440,6 @@
 
     for p in range(1, 8):
         reduce_copy(p).start()
-
-    cells_copy.wait()
-    padded[...] = jnp.concatenate(
-        [cells[...], jnp.full((TILES, 32), -1, jnp.int32)], axis=1
-    )
-    slot = lax.broadcasted_iota(jnp.int32, (128, 512), 0)
-
-    def one_hot(t, _):
-        cell = padded[pl.ds(t, 1), :]
-        high[t] = jnp.where(slot == (cell >> 7), 1.0, 0.0).astype(jnp.bfloat16)
-        low[t] = jnp.where(slot == (cell & 127), 1.0, 0.0).astype(jnp.bfloat16)
-        return 0
-
-    lax.fori_loop(0, TILES, one_hot, 0)
 
     summed = partial[me]
     for p in range(1, 8):
@@ -435,7 +491,7 @@
             pltpu.make_async_copy(arrived.at[t], arrived.at[t], recv_sem.at[t]).wait()
         for t in sources:
             value = arrived[t]
-            for _ in range(3):
+            for _ in range(2):
                 piece = value.astype(jnp.bfloat16)
                 value = value - piece.astype(jnp.float32)
                 spread = high[t] * jnp.broadcast_to(piece, (128, 512))
@@ -448,17 +504,14 @@
     sums = lax.fori_loop(0, TILES // 4, accumulate, jnp.zeros((128, 128), jnp.float32))
     flux[...] = sums[: OWNED // 128]
 
-    def finish_edges(k, _):
-        for copy in edge_copies(k, 1, *edges1) + edge_copies(k, 0, *edges0):
+    for group in range(6):
+        for copy in edge_copies(group, 1, *edges1) + edge_copies(group, 0, *edges0):
             copy.wait_send()
-        return 0
-
-    lax.fori_loop(0, LEV, finish_edges, 0)
 
     @pl.when(lev > 0)
     def _():
-        copy1.wait_send()
-        copy0.wait_send()
+        for copy in level_copies(forcing, halo1, 1) + level_copies(field, halo0, 0):
+            copy.wait_send()
 
     for p in range(1, 8):
         reduce_copy(p).wait_send()
@@ -518,7 +571,7 @@
             pltpu.VMEM((TILES, 128, 512), bf16),
             pltpu.VMEM((TILES, 128, 512), bf16),
         ]
-        + [dma((5, LEV)), dma((4,)), dma((2,)), dma((2,)), dma((2, 2, LEV)), dma((2, 2, LEV))]
+        + [dma((5, LEV // 2)), dma((4,)), dma((2, 3)), dma((2, 3)), dma((2, 2, 6)), dma((2, 2, 6))]
         + [dma((7,)), dma((7,)), dma((TILES,)), dma((TILES,))]
         + [pltpu.SemaphoreType.REGULAR((5,))],
         compiler_params=pltpu.CompilerParams(

time: 46.7 us -> 43.3 us (0.927)
  the two profiles are of different devices: /device:TPU:7 before, /device:TPU:1 now
where the time goes in v4:
time: 43.3 us; the launch traced here: 43.2 us
  Pallas kernels  42.5 us (98%)
  between operations  0.64 us (1%)
    pallas_call x1, Pallas kernels, shards(): pl.pallas_call(adjoint_kernel, out_shape=(shape(forcing.shape, f32), shap...  40.4 us
    pallas_call x1, Pallas kernels, shards(): pl.pallas_call(store_kernel, out_shape=(shape(forcing.shape, f32), shape(...  2.11 us

profile of v4, /device:TPU:1, one launch (start us, length us, event | category | flops | bytes accessed | tf_op | source)
XLA Modules:
  0.0 43.2 jit_solution(4283159909377654819)
XLA Ops:
  0.6 40.4 %adjoint.1 = (f32[4,18,40,384]{3,2,1,0:T(8,128)S(1)}, f32[120,128]{1,0:T(8,128)S(1)}) custom-call(s32[2,32]{1,0:T(2,128)} %bitcast.2, f32[18]{0:T(128)} %level_weight.1, f32[4,18,40,384]{3,2,1,0:T(8,128)} %forcing.1, bf16[18,40,384]{2,1,0:T(8,128)(2,1)} %courant_x.1, bf16[18,40,384]{2,1,0:T(8,128)(2,1)} %courant_y.1, bf16[18,40,384]{2,1,0:T(8,128)(2,1)} %mass_flux.1, ...), custom_call_target="tpu_custom_call" | custom-call | tf_op jit(solution)/shard_map/adjoint/pallas_call | solution.py:549
  41.1 2.1 %store.1 = (f32[4,18,40,384]{3,2,1,0:T(8,128)}, f32[120,128]{1,0:T(8,128)}) custom-call(f32[4,18,40,384]{3,2,1,0:T(8,128)S(1)} %get-tuple-element.6.adjoint, f32[120,128]{1,0:T(8,128)S(1)} %get-tuple-element.7.flux), custom_call_target="tpu_custom_call" | custom-call | tf_op jit(solution)/shard_map/store/pallas_call | solution.py:590

commit v5 on v4

--- a/solution.py
+++ b/solution.py
@@ -18,8 +18,7 @@
 LIMIT_FIRST = 40
 LIMIT_SECOND = 8
 CHUNKS = ((0, 16), (16, 16), (32, 8))
-PARTS = ((0, 8), (32, 8), (8, 24))
-EDGE1_AT, EDGE0_AT, REST0_AT = 0, 0, 2
+REST0_AT = 1
 
 
 def coefficients(courant, code, bit):
@@ -101,6 +100,8 @@
     padded,
     halo1,
     halo0,
+    rows_out,
+    rows_in,
     first1,
     last1,
     left1,
@@ -188,14 +189,17 @@
         copy.start()
 
     def level_copies(source, halo, step):
-        return [
+        return (
             pltpu.make_async_remote_copy(
-                source.at[:, 0, pl.ds(start, size)], halo.at[:, pl.ds(start, size)],
-                lev_send.at[step, i], lev_recv.at[step, i],
+                rows_out.at[step], rows_in.at[step],
+                lev_send.at[step, 0], lev_recv.at[step, 0],
                 device_id={"lev": lower}, device_id_type=MESH,
-            )
-            for i, (start, size) in enumerate(PARTS)
-        ]
+            ),
+            pltpu.make_async_remote_copy(
+                source.at[:, 0], halo, lev_send.at[step, 1], lev_recv.at[step, 1],
+                device_id={"lev": lower}, device_id_type=MESH,
+            ),
+        )
 
     def edge_copies(group, step, first, last, left, right):
         if isinstance(group, int) and group >= 4:
@@ -216,6 +220,10 @@
         )
 
     def start_levels(source, halo, step):
+        for i, row in enumerate((0, ROWS - 1)):
+            for s in range(SEC):
+                rows_out[step, i, s : s + 1, :] = field[s, 0, row : row + 1, :]
+
         @pl.when(lev > 0)
         def _():
             for copy in level_copies(source, halo, step):
@@ -227,8 +235,8 @@
 
         start_levels(forcing, halo1, 1)
 
-    def vertical_second(k, above, bit, step, first, last, left, right, chunks=CHUNKS):
-        for start, size in chunks:
+    def vertical_second(k, above, bit, step, first, last, left, right, rims_too=True):
+        for start, size in CHUNKS:
             rows = slice(start, start + size)
             mixing = mf[k, rows, :].astype(jnp.float32)
             ahead, back, centre = second_coefficients(
@@ -243,9 +251,9 @@
                     + back * pltpu.roll(value, 1, 1)
                 )
                 swept[s, k, rows, :] = value
-                if start == 0:
+                if rims_too and start == 0:
                     first[k, s : s + 1, :] = value[:1]
-                if start == 32:
+                if rims_too and start == 32:
                     last[k, s : s + 1, :] = value[7:]
 
     def send_edges(group, step, edges):
@@ -287,25 +295,45 @@
     inner_level(16, step1)
     send_edges(4, 1, edges1)
 
-    def top_level(source, halo, step, step_args, parts):
-        copies = level_copies(source, halo, step)
-
+    def top_level(source, halo, step, step_args):
         @pl.when(lev < 3)
         def _():
-            for i in parts:
-                copies[i].wait_recv()
+            level_copies(source, halo, step)[1].wait_recv()
 
         @pl.when(lev == 3)
         def _():
-            for i in parts:
-                start, size = PARTS[i]
-                for s in range(SEC):
-                    halo[s, start : start + size] = field[s, LEV - 1, start : start + size]
+            for s in range(SEC):
+                halo[s] = field[s, LEV - 1]
 
         vertical_second(
-            LEV - 1, lambda s, rows: halo[s, rows, :], *step_args,
-            chunks=[PARTS[i] for i in parts],
+            LEV - 1, lambda s, rows: halo[s, rows, :], *step_args, rims_too=False
         )
+
+    def top_rims(source, halo, step, bit, targets):
+        @pl.when(lev < 3)
+        def _():
+            level_copies(source, halo, step)[0].wait_recv()
+
+        for i, (start, at, target) in enumerate(((0, 0, targets[0]), (32, 7, targets[1]))):
+            rows = slice(start, start + 8)
+            value = jnp.concatenate(
+                [field[s, LEV - 1, start + at : start + at + 1, :] for s in range(SEC)], axis=0
+            )
+            ahead, back, centre = second_coefficients(
+                cy[LEV - 1, rows, :].astype(jnp.float32), code[LEV - 1, rows, :], bit
+            )
+            mixing = mf[LEV - 1, rows, :].astype(jnp.float32)
+            ahead, back, centre, mixing = [
+                x[at : at + 1] for x in (ahead, back, centre, mixing)
+            ]
+            above = jnp.where(lev == 3, value, rows_in[step, i])
+            value = value + mixing * (above - value)
+            target[LEV - 1] = (
+                centre * value
+                + ahead * pltpu.roll(value, COLS - 1, 1)
+                + back * pltpu.roll(value, 1, 1)
+            )
+        send_edges(5, step, edges1 if step else edges0)
 
     cells_copy.wait()
     padded[...] = jnp.concatenate(
@@ -339,11 +367,12 @@
     hear(0)
     tell(1)
 
-    def first_group(g):
-        take_edges(g, 1, edges1)
-        for i in range(2):
-            loads(2 * g + i)[4].wait()
-        for j in range(4):
+    def first_group(g, least=0):
+        if least == 0:
+            take_edges(g, 1, edges1)
+            for i in range(2):
+                loads(2 * g + i)[4].wait()
+        for j in range(least, 4):
             first_dimension(4 * g + j, edges1, 2, field)
 
     def second_group(g):
@@ -351,28 +380,17 @@
             inner_level(4 * g + j, step0)
         send_edges(g, 0, edges0)
 
-    def early_top1():
-        top_level(forcing, halo1, 1, step1, (0, 1))
-        send_edges(5, 1, edges1)
-
-    def early_top0():
-        take_edges(5, 1, edges1)
-        first_dimension(17, edges1, 2, field)
-        inner_level(16, step0)
-        send_edges(4, 0, edges0)
-        top_level(field, halo0, 0, step0, (0, 1))
-        send_edges(5, 0, edges0)
-
-    first_group(0)
+    top_rims(forcing, halo1, 1, 3, (first1, last1))
+    take_edges(0, 1, edges1)
+    for i in range(2):
+        loads(i)[4].wait()
+    first_dimension(0, edges1, 2, field)
     start_levels(field, halo0, 0)
+    first_group(0, 1)
 
     def phase_b(g, _):
         first_group(g + 1)
         second_group(g)
-
-        @pl.when(g == EDGE1_AT)
-        def _():
-            early_top1()
 
         @pl.when(g == 1)
         def _():
@@ -388,7 +406,12 @@
     second_group(3)
     hear(2)
     tell(3)
-    top_level(forcing, halo1, 1, step1, (2,))
+    top_level(forcing, halo1, 1, step1)
+    take_edges(5, 1, edges1)
+    first_dimension(17, edges1, 2, field)
+    top_rims(field, halo0, 0, 1, (first0, last0))
+    inner_level(16, step0)
+    send_edges(4, 0, edges0)
 
     share_copy.wait()
     weight_copy.wait()
@@ -404,13 +427,9 @@
             total[rows, :] += weight[k] * term
 
     def phase_c(g, _):
-        @pl.when(g == EDGE0_AT)
-        def _():
-            early_top0()
-
         @pl.when(g == REST0_AT)
         def _():
-            top_level(field, halo0, 0, step0, (2,))
+            top_level(field, halo0, 0, step0)
 
         @pl.when(g == 1)
         def _():
@@ -561,6 +580,7 @@
         + [plane]
         + [pltpu.VMEM((TILES, 480), i32), pltpu.VMEM((TILES, 512), i32)]
         + [plane] * 2
+        + [pltpu.VMEM((2, 2, SEC, COLS), f32)] * 2
         + [edge] * 8
         + [
             pltpu.VMEM((ROWS, COLS), f32),
@@ -571,7 +591,7 @@
             pltpu.VMEM((TILES, 128, 512), bf16),
             pltpu.VMEM((TILES, 128, 512), bf16),
         ]
-        + [dma((5, LEV // 2)), dma((4,)), dma((2, 3)), dma((2, 3)), dma((2, 2, 6)), dma((2, 2, 6))]
+        + [dma((5, LEV // 2)), dma((4,)), dma((2, 2)), dma((2, 2)), dma((2, 2, 6)), dma((2, 2, 6))]
         + [dma((7,)), dma((7,)), dma((TILES,)), dma((TILES,))]
         + [pltpu.SemaphoreType.REGULAR((5,))],
         compiler_params=pltpu.CompilerParams(

time: 43.3 us -> 41.8 us (0.965)
  Pallas kernels: 42.5 us -> 41.1 us
    pallas_call x1, Pallas kernels: 40.4 us -> 39 us  [shards(): pl.pallas_call(adjoint_kernel, out_shape=(shape(forcing.shape, f32), shap...]
where the time goes in v5:
time: 41.8 us; the launch traced here: 41.7 us
  Pallas kernels  41.1 us (98%)
  between operations  0.64 us (2%)
    pallas_call x1, Pallas kernels, shards(): pl.pallas_call(adjoint_kernel, out_shape=(shape(forcing.shape, f32), shap...  39 us
    pallas_call x1, Pallas kernels, shards(): pl.pallas_call(store_kernel, out_shape=(shape(forcing.shape, f32), shape(...  2.11 us

profile of v5, /device:TPU:1, one launch (start us, length us, event | category | flops | bytes accessed | tf_op | source)
XLA Modules:
  0.0 41.7 jit_solution(13074119009843766396)
XLA Ops:
  0.6 39.0 %adjoint.1 = (f32[4,18,40,384]{3,2,1,0:T(8,128)S(1)}, f32[120,128]{1,0:T(8,128)S(1)}) custom-call(s32[2,32]{1,0:T(2,128)} %bitcast.2, f32[18]{0:T(128)} %level_weight.1, f32[4,18,40,384]{3,2,1,0:T(8,128)} %forcing.1, bf16[18,40,384]{2,1,0:T(8,128)(2,1)} %courant_x.1, bf16[18,40,384]{2,1,0:T(8,128)(2,1)} %courant_y.1, bf16[18,40,384]{2,1,0:T(8,128)(2,1)} %mass_flux.1, ...), custom_call_target="tpu_custom_call" | custom-call | tf_op jit(solution)/shard_map/adjoint/pallas_call | solution.py:568
  39.6 2.1 %store.1 = (f32[4,18,40,384]{3,2,1,0:T(8,128)}, f32[120,128]{1,0:T(8,128)}) custom-call(f32[4,18,40,384]{3,2,1,0:T(8,128)S(1)} %get-tuple-element.6.adjoint, f32[120,128]{1,0:T(8,128)S(1)} %get-tuple-element.7.flux), custom_call_target="tpu_custom_call" | custom-call | tf_op jit(solution)/shard_map/store/pallas_call | solution.py:610

commit v6 on v5

--- a/solution.py
+++ b/solution.py
@@ -497,6 +497,26 @@
     hear(4)
     lax.fori_loop(0, TILES, send, 0)
 
+    for group in range(6):
+        for copy in edge_copies(group, 1, *edges1) + edge_copies(group, 0, *edges0):
+            copy.wait_send()
+
+    @pl.when(lev > 0)
+    def _():
+        for copy in level_copies(forcing, halo1, 1) + level_copies(field, halo0, 0):
+            copy.wait_send()
+
+    for p in range(1, 8):
+        reduce_copy(p).wait_send()
+
+    def finish(i, _):
+        @pl.when(jnp.logical_not(is_self(i)))
+        def _():
+            send_copy(i).wait_send()
+        return 0
+
+    lax.fori_loop(0, TILES, finish, 0)
+
     def step_of(a):
         return a + a // 2 - 2 * (a // 3)
 
@@ -522,26 +542,6 @@
 
     sums = lax.fori_loop(0, TILES // 4, accumulate, jnp.zeros((128, 128), jnp.float32))
     flux[...] = sums[: OWNED // 128]
-
-    for group in range(6):
-        for copy in edge_copies(group, 1, *edges1) + edge_copies(group, 0, *edges0):
-            copy.wait_send()
-
-    @pl.when(lev > 0)
-    def _():
-        for copy in level_copies(forcing, halo1, 1) + level_copies(field, halo0, 0):
-            copy.wait_send()
-
-    for p in range(1, 8):
-        reduce_copy(p).wait_send()
-
-    def finish(i, _):
-        @pl.when(jnp.logical_not(is_self(i)))
-        def _():
-            send_copy(i).wait_send()
-        return 0
-
-    lax.fori_loop(0, TILES, finish, 0)
 
 
 def store_kernel(adjoint, flux, adjoint_out, flux_out, sem):

time: 41.8 us -> 41.3 us (0.988)
  Pallas kernels: 41.1 us -> 40.6 us
    pallas_call x1, Pallas kernels: 39 us -> 38.5 us  [shards(): pl.pallas_call(adjoint_kernel, out_shape=(shape(forcing.shape, f32), shap...]
where the time goes in v6:
time: 41.3 us; the launch traced here: 41.2 us
  Pallas kernels  40.6 us (98%)
  between operations  0.64 us (2%)
    pallas_call x1, Pallas kernels, shards(): pl.pallas_call(adjoint_kernel, out_shape=(shape(forcing.shape, f32), shap...  38.5 us
    pallas_call x1, Pallas kernels, shards(): pl.pallas_call(store_kernel, out_shape=(shape(forcing.shape, f32), shape(...  2.11 us

profile of v6, /device:TPU:1, one launch (start us, length us, event | category | flops | bytes accessed | tf_op | source)
XLA Modules:
  0.0 41.2 jit_solution(12014289020347047047)
XLA Ops:
  0.6 38.5 %adjoint.1 = (f32[4,18,40,384]{3,2,1,0:T(8,128)S(1)}, f32[120,128]{1,0:T(8,128)S(1)}) custom-call(s32[2,32]{1,0:T(2,128)} %bitcast.2, f32[18]{0:T(128)} %level_weight.1, f32[4,18,40,384]{3,2,1,0:T(8,128)} %forcing.1, bf16[18,40,384]{2,1,0:T(8,128)(2,1)} %courant_x.1, bf16[18,40,384]{2,1,0:T(8,128)(2,1)} %courant_y.1, bf16[18,40,384]{2,1,0:T(8,128)(2,1)} %mass_flux.1, ...), custom_call_target="tpu_custom_call" | custom-call | tf_op jit(solution)/shard_map/adjoint/pallas_call | solution.py:568
  39.1 2.1 %store.1 = (f32[4,18,40,384]{3,2,1,0:T(8,128)}, f32[120,128]{1,0:T(8,128)}) custom-call(f32[4,18,40,384]{3,2,1,0:T(8,128)S(1)} %get-tuple-element.6.adjoint, f32[120,128]{1,0:T(8,128)S(1)} %get-tuple-element.7.flux), custom_call_target="tpu_custom_call" | custom-call | tf_op jit(solution)/shard_map/store/pallas_call | solution.py:610

commit v7 on v6

--- a/solution.py
+++ b/solution.py
@@ -169,8 +169,8 @@
 
     beside_z = [tile_at(along_z + i, along_x, core) for i in (1, 3)]
     beside_x = [tile_at(along_z, along_x + i, core) for i in (1, 3)]
-    near = [{"tile": after}, {"tile": before}] + beside_z + beside_x
-    near += [member(lax.rem(me + p, 8)) for p in range(1, 8)]
+    near = [member(lax.rem(me + p, 8)) for p in range(1, 8)]
+    near += [{"tile": after}, {"tile": before}] + beside_z + beside_x
     for device in near:
         pl.semaphore_signal(barrier, inc=1, device_id=device, device_id_type=MESH)
 
@@ -470,17 +470,22 @@
             pair = pltpu.roll(pair, 768 - 96 * r, 1)
         outgoing[r] = pair[:, :512]
 
+    def goal(i):
+        return me * 4 + lax.rem(i, 4), lax.rem(lev + 2 + i // 8, 4), lax.rem(i // 4, 2)
+
     def send_copy(i):
+        to_tile, to_lev, to_sec = goal(i)
         return pltpu.make_async_remote_copy(
-            outgoing.at[i // 8], arrived.at[tile], send_sem.at[i], recv_sem.at[tile],
-            device_id={
-                "tile": me * 4 + i // 8, "lev": lax.rem(i, 8) // 2, "sec": lax.rem(i, 2),
-            },
+            outgoing.at[lax.rem(i, 4)], arrived.at[tile], send_sem.at[i], recv_sem.at[tile],
+            device_id={"tile": to_tile, "lev": to_lev, "sec": to_sec},
             device_id_type=MESH,
         )
 
     def is_self(i):
-        return jnp.logical_and(me * 4 + i // 8 == tile, lax.rem(i, 8) == me)
+        to_tile, to_lev, to_sec = goal(i)
+        return jnp.logical_and(
+            to_tile == tile, jnp.logical_and(to_lev == lev, to_sec == sec)
+        )
 
     def send(i, _):
         @pl.when(jnp.logical_not(is_self(i)))
@@ -490,7 +495,7 @@
         @pl.when(is_self(i))
         def _():
             pltpu.make_async_copy(
-                outgoing.at[i // 8], arrived.at[tile], recv_sem.at[tile]
+                outgoing.at[lax.rem(i, 4)], arrived.at[tile], recv_sem.at[tile]
             ).start()
         return 0
 

time: 41.3 us -> 42.7 us (1.034)
  Pallas kernels: 40.6 us -> 42 us
    pallas_call x1, Pallas kernels: 38.5 us -> 39.8 us  [shards(): pl.pallas_call(adjoint_kernel, out_shape=(shape(forcing.shape, f32), shap...]
where the time goes in v7:
time: 42.7 us; the launch traced here: 42.6 us
  Pallas kernels  42 us (98%)
  between operations  0.64 us (1%)
    pallas_call x1, Pallas kernels, shards(): pl.pallas_call(adjoint_kernel, out_shape=(shape(forcing.shape, f32), shap...  39.8 us
    pallas_call x1, Pallas kernels, shards(): pl.pallas_call(store_kernel, out_shape=(shape(forcing.shape, f32), shape(...  2.11 us

profile of v7, /device:TPU:1, one launch (start us, length us, event | category | flops | bytes accessed | tf_op | source)
XLA Modules:
  0.0 42.6 jit_solution(17748283078229999929)
XLA Ops:
  0.6 39.8 %adjoint.1 = (f32[4,18,40,384]{3,2,1,0:T(8,128)S(1)}, f32[120,128]{1,0:T(8,128)S(1)}) custom-call(s32[2,32]{1,0:T(2,128)} %bitcast.2, f32[18]{0:T(128)} %level_weight.1, f32[4,18,40,384]{3,2,1,0:T(8,128)} %forcing.1, bf16[18,40,384]{2,1,0:T(8,128)(2,1)} %courant_x.1, bf16[18,40,384]{2,1,0:T(8,128)(2,1)} %courant_y.1, bf16[18,40,384]{2,1,0:T(8,128)(2,1)} %mass_flux.1, ...), custom_call_target="tpu_custom_call" | custom-call | tf_op jit(solution)/shard_map/adjoint/pallas_call | solution.py:573
  40.5 2.1 %store.1 = (f32[4,18,40,384]{3,2,1,0:T(8,128)}, f32[120,128]{1,0:T(8,128)}) custom-call(f32[4,18,40,384]{3,2,1,0:T(8,128)S(1)} %get-tuple-element.6.adjoint, f32[120,128]{1,0:T(8,128)S(1)} %get-tuple-element.7.flux), custom_call_target="tpu_custom_call" | custom-call | tf_op jit(solution)/shard_map/store/pallas_call | solution.py:615
